TPU v7x, 32 devices: a whole 2x2x4 slice. The times are simulated.
32 devices in a mesh: cols: 16 (over z, y, core), fsdp: 2 (over x).
Axes of the slice: x: 2, y: 2, z: 4, core: 2. Of those that a mesh axis runs over, the one named last changes fastest.
Arguments:
- alignment: bfloat16 [2, 2, 4, 1024, 768], P(None, 'fsdp', None, 'cols'), may hold values from -6 to 6
- cotangent: bfloat16 [2, 2, 4, 1024, 768], P(None, 'fsdp', None, 'cols'), may hold values from -6 to 6
- row_counts: int32 [2, 2], P(None, 'fsdp'), may hold values from 1 to 4, as said below
- band_reach: int32 [2, 2, 2, 1024], P(None, 'fsdp', None, 'cols'), may hold values from 0 to 32
- master_weights: float32 [12288, 768], P(('cols', 'fsdp'))
- weight_moment: float32 [12288, 768], P(('cols', 'fsdp'))
- weight_square: float32 [12288, 768], P(('cols', 'fsdp')), as said below
- norm_gains: float32 [2304], P(('cols', 'fsdp')), may hold values from 0.5 to 1.5
- gain_moment: float32 [2304], P(('cols', 'fsdp'))
- gain_square: float32 [2304], P(('cols', 'fsdp')), as said below
Outputs:
- block_output: bfloat16 [2, 2, 4, 1024, 768], P(None, 'fsdp', None, 'cols')
- input_grad: bfloat16 [2, 2, 4, 1024, 768], P(None, 'fsdp', None, 'cols')
- new_weights: float32 [12288, 768], P(('cols', 'fsdp'))
- new_moment: float32 [12288, 768], P(('cols', 'fsdp'))
- new_square: float32 [12288, 768], P(('cols', 'fsdp'))
- weight_copies: bfloat16 [12288, 768], P(('cols', 'fsdp'))
- new_gains: float32 [2304], P(('cols', 'fsdp'))
- new_gain_moment: float32 [2304], P(('cols', 'fsdp'))
- new_gain_square: float32 [2304], P(('cols', 'fsdp'))
Inputs may be any that keep to these rules, and one draw needn't show every extreme that they name: `row_counts`: every alignment holds at least one live sequence. `weight_square`: positive. `gain_square`: positive.
All inputs are finite; a program needn't handle non-finite values.
Results may differ from a plain program's by a relative error of at most 0.017.
Values may be sent and summed in bfloat16 or wider, within the bound.
No kernel may reach another device: no remote copies, remote signals or barrier semaphores. Data moves between devices by JAX's collectives and lax.ppermute only.
A program may use at most 240 MiB of HBM per device.

v0:
```python
from functools import partial

import jax
import jax.numpy as jnp
from jax import lax
from jax.experimental import pallas as pl
from jax.experimental.pallas import tpu as pltpu
from jax.sharding import PartitionSpec as P

D = 768
H = 12
DH = 64
FF = 3072
NMAT = 16
ROWS = 4
CB = 64
HALO = 32
MB = 2
EXT = CB + 2 * HALO
SEQ = MB * ROWS
TOK = SEQ * CB
PAIRS = H // 2
LANES = 128
FOLD = FF // D
SPAN = D // 2
PART = SPAN // 2
EXTRA = 16
PER_GROUP = 10

EPS = 1e-05
BETA_ONE = 0.9
BETA_TWO = 0.999
ADAM_EPS = 1e-08
DECAY = 0.01
RATE_GAIN = 0.3
STEP_NUMBER = 10.0
MASKED = -1e30
F32 = jnp.float32
LOW = jnp.bfloat16


def dot_nn(a, b):
    return lax.dot_general(a, b, (((1,), (0,)), ((), ())), preferred_element_type=F32)


def dot_nt(a, b):
    return lax.dot_general(a, b, (((1,), (1,)), ((), ())), preferred_element_type=F32)


def dot_tn(a, b):
    return lax.dot_general(a, b, (((0,), (0,)), ((), ())), preferred_element_type=F32)


def standardize(values):
    center = values - jnp.mean(values, axis=-1, keepdims=True)
    spread = lax.rsqrt(jnp.mean(center * center, axis=-1, keepdims=True) + EPS)
    return center * spread, spread


def norm_pull(upward, values, gain):
    scaled, spread = standardize(values)
    weighted = upward * gain
    result = spread * (
        weighted
        - jnp.mean(weighted, axis=-1, keepdims=True)
        - scaled * jnp.mean(weighted * scaled, axis=-1, keepdims=True)
    )
    return result, jnp.sum(upward * scaled, axis=0, keepdims=True)


def lane_window(pair):
    return pl.ds(pl.multiple_of(pair * LANES, LANES), LANES)


def side_by_side(ref, micro, window):
    return jnp.concatenate([ref[micro * ROWS + r, :, window] for r in range(ROWS)], axis=1)


def head_stack(packed):
    lane = lax.broadcasted_iota(jnp.int32, packed.shape, 1)
    first = (lane % LANES) < DH
    zero = jnp.zeros_like(packed)
    return jnp.concatenate([jnp.where(first, packed, zero), jnp.where(first, zero, packed)], axis=0)


def head_merge(stacked, r):
    block = stacked[:, r * LANES : (r + 1) * LANES]
    lane = lax.broadcasted_iota(jnp.int32, (CB, LANES), 1)
    return jnp.where(lane < DH, block[:CB], block[CB:])


def head_sums():
    feature = lax.broadcasted_iota(jnp.int32, (D, LANES), 0)
    head = lax.broadcasted_iota(jnp.int32, (D, LANES), 1)
    return (feature // DH == head).astype(F32).astype(LOW)


def head_spread():
    head = lax.broadcasted_iota(jnp.int32, (LANES, D), 0)
    feature = lax.broadcasted_iota(jnp.int32, (LANES, D), 1)
    return (feature // DH == head).astype(F32).astype(LOW)


FULL = SPAN + EXTRA
STARTS = (0, FULL, 2 * FULL, 3 * FULL, 3 * FULL + PART)


def spot(buffers, number, row):
    if len(buffers) == 5:
        return buffers[number], row
    start = STARTS[number]
    if len(buffers) == 2 and number >= 3:
        return buffers[1], start - 3 * FULL + row
    return buffers[0], start + row


def regroup(sizes, refs):
    groups, start = [], 0
    for size in sizes:
        groups.append(refs[start : start + size])
        start += size
    return groups


def fetch_matrix(place, sources, table, matrix, target, sems, base):
    y_rel = jnp.where(place[1] == matrix // 2, 0, 1)
    waits = []
    for x in range(2):
        x_rel = jnp.where(place[0] == x, 0, 1)
        block = 2 * y_rel + x_rel
        sem = sems.at[base + x]
        for index in sorted(set(table)):
            here = None
            for plane, chosen in enumerate(table):
                if chosen == index:
                    hit = place[3] == plane
                    here = hit if here is None else jnp.logical_or(here, hit)
            for core_rel in range(2):
                held = jnp.logical_and(here, place[2] == (matrix % 2) ^ core_rel)
                buffers = sources[2 * index + core_rel]
                for number in range(5):
                    source, row = spot(buffers, number, 0)
                    size = SPAN if number < 3 else PART
                    to = x * SPAN + (PART if number == 4 else 0)
                    part = pltpu.make_async_copy(
                        source.at[pl.ds(row, size)], target.at[pl.ds(to, size)], sem
                    )
                    pl.when(jnp.logical_and(held, block == min(number, 3)))(part.start)
                    if number == 0:
                        copy = part
        waits.append(copy)
    return waits


def fetch(place, sources, table, matrices, w, sems, first=0):
    waits = []
    for slot, matrix in enumerate(matrices):
        slot += first
        waits.append(
            fetch_matrix(place, sources, table, matrix, w.at[slot], sems, 2 * slot)
        )
    return waits


def settle(waits):
    for copy in waits:
        copy.wait()


def emit_matrix(place, source, matrix, n, out, sems, base):
    *keep, rest, corner = out
    core_same = place[2] == matrix % 2
    y_rel = jnp.where(place[1] == matrix // 2, 0, 1)
    waits = []
    for x in range(2):
        x_rel = jnp.where(place[0] == x, 0, 1)
        spot_rel = 2 * y_rel + x_rel
        block = source.at[pl.ds(x * SPAN, SPAN)]
        sem = sems.at[base + x]
        sent = jnp.logical_not(core_same)
        for number, target in enumerate(keep):
            kept = pltpu.make_async_copy(block, target.at[n], sem)
            pl.when(jnp.logical_and(core_same, spot_rel == number))(kept.start)
        near = pltpu.make_async_copy(block, rest.at[jnp.minimum(spot_rel, 2), n], sem)
        far = pltpu.make_async_copy(block, corner.at[n], sem)
        pl.when(jnp.logical_and(sent, spot_rel < 3))(near.start)
        pl.when(jnp.logical_and(sent, spot_rel == 3))(far.start)
        waits.append(far)
    return waits


def gain_copies(sources, group, target, sem):
    copies = []
    for core_rel in range(2):
        buffers = sources[2 * group + core_rel]
        for number, row in ((0, SPAN), (1, SPAN), (2, SPAN), (4, PART)):
            source, row = spot(buffers, number, row)
            copy = pltpu.make_async_copy(
                source.at[pl.ds(row, EXTRA)], target.at[len(copies)], sem.at[len(copies)]
            )
            copies.append(copy)
    return copies


def row_project(
    spec, count, scal, place, tokens, from_low, from_high, *refs
):
    table, group = spec
    sources, (a1e, q, ke, ve, gain, w, held, sems, gain_sems) = regroup(count, refs), refs[sum(count) :]
    parts = gain_copies(sources, group, held, gain_sems)
    for copy in parts:
        copy.start()
    copies = fetch(place, sources, table, range(3), w, sems)
    settle(parts)
    total = held[0].astype(F32)
    for k in range(1, 8):
        total = total + held[k].astype(F32)
    gain[...] = total[:3]

    def norm_step(i, _):
        for source, start, size in (
            (from_low, 0, HALO),
            (tokens, HALO, CB),
            (from_high, HALO + CB, HALO),
        ):
            scaled, _s = standardize(source[i].astype(F32))
            a1e[i, start : start + size] = (scaled * gain[0:1]).astype(LOW)
        return 0

    lax.fori_loop(0, SEQ, norm_step, 0, unroll=True)
    wide = a1e[...].reshape(SEQ * EXT, D)
    settle(copies[1])
    ke[...] = dot_nn(wide, w[1]).astype(LOW).reshape(SEQ, EXT, D)
    settle(copies[2])
    ve[...] = dot_nn(wide, w[2]).astype(LOW).reshape(SEQ, EXT, D)
    inner = a1e[:, HALO : HALO + CB, :].reshape(TOK, D)
    settle(copies[0])
    q[...] = dot_nn(inner, w[0]).astype(LOW).reshape(SEQ, CB, D)
    for i in range(SEQ):
        q[i] = (q[i].astype(F32) * scal[i // ROWS, 1 + i % ROWS]).astype(LOW)


def row_attend(
    table, count, scal, place, tokens, q, ke, ve, allowed, gain, *refs
):
    sources, (p1, o1, x1, a2, w, sems) = regroup(count, refs), refs[sum(count) :]
    copies = fetch(place, sources, table, (3,), w, sems)

    def attend(pair, _):
        window = lane_window(pair)
        for m in range(MB):
            query = head_stack(side_by_side(q, m, window))
            scores = dot_nt(query, side_by_side(ke, m, window)) * scal[m, 0]
            mask = allowed[m]
            mask = jnp.concatenate([mask, mask], axis=0)
            scores = jnp.where(mask > 0, scores, MASKED)
            weight = jnp.exp(scores - jnp.max(scores, axis=-1, keepdims=True))
            prob = weight / jnp.sum(weight, axis=-1, keepdims=True)
            p1[m, pair] = prob
            mixed = dot_nn(prob.astype(LOW), side_by_side(ve, m, window))
            for r in range(ROWS):
                o1[m * ROWS + r, :, window] = head_merge(mixed, r).astype(LOW)
        return 0

    lax.fori_loop(0, PAIRS, attend, 0, unroll=True)
    settle(copies[0])
    x1[...] = tokens[...].astype(F32) + dot_nn(o1[...].reshape(TOK, D), w[0]).reshape(SEQ, CB, D)

    def next_norm(i, _):
        scaled, _s = standardize(x1[i])
        a2[i] = (scaled * gain[1:2]).astype(LOW)
        return 0

    lax.fori_loop(0, SEQ, next_norm, 0, unroll=True)


def col_forward(table, count, scal, place, x1, a2, gain, *refs):
    sources, (q2, k2, v2, p2, o2, x2, a3, w, sems) = regroup(count, refs), refs[sum(count) :]
    copies = fetch(place, sources, table, range(4), w, sems)
    for j in range(3):
        settle(copies[j])
    flat = a2[...].reshape(TOK, D)
    q2[...] = dot_nn(flat, w[0]).astype(LOW).reshape(SEQ, CB, D)
    k2[...] = dot_nn(flat, w[1]).astype(LOW).reshape(SEQ, CB, D)
    v2[...] = dot_nn(flat, w[2]).astype(LOW).reshape(SEQ, CB, D)
    sums = head_sums()
    spread = head_spread()

    def attend(i, _):
        micro = i // ROWS
        query = q2[i].astype(F32)
        products = jnp.concatenate(
            [(query * k2[micro * ROWS + s].astype(F32)).astype(LOW) for s in range(ROWS)], axis=0
        )
        scores = dot_nn(products, sums) * (DH ** (-0.5))
        parts = [
            jnp.where(scal[micro, 1 + s] > 0, scores[s * CB : (s + 1) * CB], MASKED)
            for s in range(ROWS)
        ]
        top = jnp.maximum(jnp.maximum(parts[0], parts[1]), jnp.maximum(parts[2], parts[3]))
        parts = [jnp.exp(part - top) for part in parts]
        scale = 1.0 / (parts[0] + parts[1] + parts[2] + parts[3])
        prob = jnp.concatenate([part * scale for part in parts], axis=0)
        p2[i] = prob
        wide = dot_nn(prob.astype(LOW), spread)
        total = wide[:CB] * v2[micro * ROWS].astype(F32)
        for s in range(1, ROWS):
            total = total + wide[s * CB : (s + 1) * CB] * v2[micro * ROWS + s].astype(F32)
        o2[i] = total.astype(LOW)
        return 0

    lax.fori_loop(0, SEQ, attend, 0, unroll=True)
    settle(copies[3])
    x2[...] = x1[...] + dot_nn(o2[...].reshape(TOK, D), w[3]).reshape(SEQ, CB, D)

    def next_norm(i, _):
        scaled, _s = standardize(x2[i])
        a3[i] = (scaled * gain[2:3]).astype(LOW)
        return 0

    lax.fori_loop(0, SEQ, next_norm, 0, unroll=True)


CHUNK = 256


def feed_forward(tables, count, scal, place, x2, a3, cot, gain, *refs):
    sources, refs = regroup(count, refs), refs[sum(count) :]
    out, e2, dgain, *terms_out, up, down, live_cot, gl, dhd, w, dw, in_sems, out_sems = refs
    copies = []
    for n in range(2):
        copies += fetch(place, sources, tables[n], range(4), w, in_sems, 4 * n)
    for i in range(SEQ):
        live_cot[i * CB : (i + 1) * CB] = (
            cot[i].astype(F32) * scal[i // ROWS, 1 + i % ROWS]
        ).astype(LOW)
    normed = a3[...].reshape(TOK, D)
    grad = live_cot[...]
    waits = []
    for step in range(FOLD):
        settle(copies[step])
        settle(copies[FOLD + step])
        win = w[step]
        wout = w[FOLD + step]
        for base in range(0, TOK, CHUNK):
            rows = slice(base, base + CHUNK)
            hidden = dot_nn(normed[rows], win)
            pulled = dot_nt(grad[rows], wout)
            half = 0.5 * lax.erf(hidden * (0.5**0.5)) + 0.5
            gl[rows] = (hidden * half).astype(LOW)
            slope = half + hidden * (jnp.exp(-0.5 * hidden * hidden) * ((2.0 * jnp.pi) ** -0.5))
            dhd[rows] = (pulled * slope).astype(LOW)
        for n, value in enumerate((dot_tn(normed, dhd[...]), dot_tn(gl[...], grad))):
            slot = 4 * n + step
            dw[slot] = value.astype(LOW)
            waits += emit_matrix(place, dw.at[slot], step, n, terms_out, out_sems, 2 * slot)
        forward = dot_nn(gl[...], wout)
        backward = dot_nt(dhd[...], win)
        if step == 0:
            up[...] = forward
            down[...] = backward
        else:
            up[...] += forward
            down[...] += backward
    total = jnp.zeros((1, D), F32)
    for i in range(SEQ):
        rows = slice(i * CB, (i + 1) * CB)
        value = x2[i]
        out[i] = ((value + up[rows]) * scal[i // ROWS, 1 + i % ROWS]).astype(LOW)
        part, gain_part = norm_pull(down[rows], value, gain[2:3])
        e2[i] = live_cot[rows].astype(F32) + part
        total = total + gain_part
    dgain[...] = total
    settle(waits)


def col_attend_back(table, count, scal, place, e2, q2, k2, v2, p2, *refs):
    sources, refs = regroup(count, refs), refs[sum(count) :]
    dq2, dk2, dv2, do2, dka, dva, w, in_sems = refs
    copies = fetch(place, sources, table, (3,), w, in_sems)
    low = e2[...].reshape(TOK, D).astype(LOW)
    settle(copies[0])
    do2[...] = dot_nt(low, w[0]).astype(LOW).reshape(SEQ, CB, D)
    sums = head_sums()
    spread = head_spread()
    dka[...] = jnp.zeros_like(dka)
    dva[...] = jnp.zeros_like(dva)

    def pull(i, _):
        micro = i // ROWS
        upward = do2[i].astype(F32)
        products = jnp.concatenate(
            [(upward * v2[micro * ROWS + s].astype(F32)).astype(LOW) for s in range(ROWS)], axis=0
        )
        dprob = dot_nn(products, sums)
        prob = p2[i]
        mixed = prob * dprob
        inner = mixed[:CB] + mixed[CB : 2 * CB] + mixed[2 * CB : 3 * CB] + mixed[3 * CB :]
        dscore = prob * (dprob - jnp.concatenate([inner] * ROWS, axis=0))
        wide = dot_nn(prob.astype(LOW), spread)
        dwide = dot_nn(dscore.astype(LOW), spread)
        query = q2[i].astype(F32)
        total = jnp.zeros((CB, D), F32)
        for s in range(ROWS):
            rows = slice(s * CB, (s + 1) * CB)
            total = total + dwide[rows] * k2[micro * ROWS + s].astype(F32)
            dka[micro * ROWS + s] += dwide[rows] * query
            dva[micro * ROWS + s] += wide[rows] * upward
        dq2[i] = (total * (DH ** (-0.5))).astype(LOW)
        return 0

    lax.fori_loop(0, SEQ, pull, 0, unroll=True)
    dk2[...] = (dka[...] * (DH ** (-0.5))).astype(LOW)
    dv2[...] = dva[...].astype(LOW)


def col_project_back(table, count, scal, place, e2, o2, dq2, dk2, dv2, a2, x1, gain, *refs):
    sources, refs = regroup(count, refs), refs[sum(count) :]
    e1, dgain, *terms_out, acc, w, dw, in_sems, out_sems = refs
    copies = fetch(place, sources, table, range(3), w, in_sems)
    flat = a2[...].reshape(TOK, D)
    low = e2[...].reshape(TOK, D).astype(LOW)
    dw[3] = dot_tn(o2[...].reshape(TOK, D), low).astype(LOW)
    waits = emit_matrix(place, dw.at[3], 3, 0, terms_out, out_sems, 6)
    for j, ref in enumerate((dq2, dk2, dv2)):
        grads = ref[...].reshape(TOK, D)
        dw[j] = dot_tn(flat, grads).astype(LOW)
        waits += emit_matrix(place, dw.at[j], j, 0, terms_out, out_sems, 2 * j)
        settle(copies[j])
        part = dot_nt(grads, w[j]).reshape(SEQ, CB, D)
        if j == 0:
            acc[...] = part
        else:
            acc[...] += part
    gain_total = jnp.zeros((1, D), F32)
    for i in range(SEQ):
        part, gain_part = norm_pull(acc[i], x1[i], gain[1:2])
        e1[i] = e2[i] + part
        gain_total = gain_total + gain_part
    dgain[...] = gain_total
    settle(waits)


def row_backward(table, count, scal, place, e1, o1, q, ke, ve, p1, a1e, *refs):
    sources, refs = regroup(count, refs), refs[sum(count) :]
    dq, dke, dve, *terms_out, do1, w, dw, in_sems, out_sems = refs
    copies = fetch(place, sources, table, (3,), w, in_sems)
    low = e1[...].reshape(TOK, D).astype(LOW)
    settle(copies[0])
    do1[...] = dot_nt(low, w[0]).astype(LOW).reshape(SEQ, CB, D)

    def pull(pair, _):
        window = lane_window(pair)
        for m in range(MB):
            query = head_stack(side_by_side(q, m, window))
            upward = head_stack(side_by_side(do1, m, window))
            prob = p1[m, pair]
            dprob = dot_nt(upward, side_by_side(ve, m, window))
            dscore = prob * (dprob - jnp.sum(prob * dprob, axis=-1, keepdims=True))
            dscore = dscore.astype(LOW)
            dvalue = dot_tn(prob.astype(LOW), upward)
            dkey = dot_tn(dscore, query) * scal[m, 0]
            dquery = dot_nn(dscore, side_by_side(ke, m, window)) * scal[m, 0]
            for r in range(ROWS):
                lanes = slice(r * LANES, (r + 1) * LANES)
                dve[m * ROWS + r, :, window] = dvalue[:, lanes].astype(LOW)
                dke[m * ROWS + r, :, window] = dkey[:, lanes].astype(LOW)
                dq[m * ROWS + r, :, window] = (head_merge(dquery, r) * scal[m, 1 + r]).astype(LOW)
        return 0

    lax.fori_loop(0, PAIRS, pull, 0, unroll=True)
    wide = a1e[...].reshape(SEQ * EXT, D)
    own = a1e[:, HALO : HALO + CB, :].reshape(TOK, D)
    waits = []
    for j, (left, right) in enumerate(
        (
            (own, dq[...].reshape(TOK, D)),
            (wide, dke[...].reshape(SEQ * EXT, D)),
            (wide, dve[...].reshape(SEQ * EXT, D)),
            (o1[...].reshape(TOK, D), low),
        )
    ):
        dw[j] = dot_tn(left, right).astype(LOW)
        waits += emit_matrix(place, dw.at[j], j, 0, terms_out, out_sems, 2 * j)
    settle(waits)


def input_project(
    table, count, scal, place, dq, dke, dve, tokens, from_low, from_high, *refs
):
    sources, (inner, to_low, to_high, dgain, acc, w, sems) = regroup(count, refs), refs[sum(count) :]
    copies = fetch(place, sources, table, range(3), w, sems)
    settle(copies[1])
    acc[...] = dot_nt(dke[...].reshape(SEQ * EXT, D), w[1]).reshape(SEQ, EXT, D)
    settle(copies[2])
    acc[...] += dot_nt(dve[...].reshape(SEQ * EXT, D), w[2]).reshape(SEQ, EXT, D)
    settle(copies[0])
    acc[:, HALO : HALO + CB, :] += dot_nt(dq[...].reshape(TOK, D), w[0]).reshape(SEQ, CB, D)
    total = jnp.zeros((1, D), F32)
    for i in range(SEQ):
        for source, start, size in (
            (from_low, 0, HALO),
            (tokens, HALO, CB),
            (from_high, HALO + CB, HALO),
        ):
            scaled, _s = standardize(source[i].astype(F32))
            total = total + jnp.sum(acc[i, start : start + size] * scaled, axis=0, keepdims=True)
    dgain[...] = total
    inner[...] = acc[:, HALO : HALO + CB, :]
    to_low[...] = acc[:, :HALO, :].astype(LOW)
    to_high[...] = acc[:, HALO + CB :, :].astype(LOW)


def input_finish(inner, from_low, from_high, e1, tokens, gain, grad):
    def step(i, _):
        upward = jnp.concatenate(
            [
                inner[i, :HALO] + from_low[i].astype(F32),
                inner[i, HALO:] + from_high[i].astype(F32),
            ],
            axis=0,
        )
        part, _g = norm_pull(upward, tokens[i].astype(F32), gain[0:1])
        grad[i] = (e1[i] + part).astype(LOW)
        return 0

    lax.fori_loop(0, SEQ, step, 0, unroll=True)


def in_vmem(count):
    return [pl.BlockSpec(memory_space=pltpu.VMEM)] * count


def like(*shapes):
    return tuple(jax.ShapeDtypeStruct(shape, dtype) for shape, dtype in shapes)


SEQ_CB = (SEQ, CB, D)
SEQ_EXT = (SEQ, EXT, D)
RIM = (SEQ, HALO, D)
PER_MICRO = 1.15e9
VM = pltpu.VMEM
DMA = pltpu.SemaphoreType.DMA


ROOM = {col_attend_back: 40, col_project_back: 40, row_backward: 40, input_project: 40, input_finish: 40}


def pieces(count):
    return (
        *(((count, SPAN, D), LOW),) * 4,
        ((3, count, SPAN, D), LOW),
        ((count, SPAN, D), LOW),
    )


def run_kernel(body, scalars, args, weights, outs, raw_out, scratch, micros):
    vmem = pl.BlockSpec(memory_space=pltpu.VMEM)
    raw = pl.BlockSpec(memory_space=pltpu.HBM)
    moved = sum(a.size * a.dtype.itemsize for a in args)
    moved += sum(o.size * jnp.dtype(o.dtype).itemsize for o in outs)
    call = body
    sources = ()
    if weights is not None:
        table, groups = weights
        sources = [buffer for group in groups for buffer in group]
        call = partial(body, table, tuple(len(group) for group in groups))
    return pl.pallas_call(
        call,
        name=body.__name__,
        out_shape=outs,
        in_specs=[pl.BlockSpec(memory_space=pltpu.SMEM)] * len(scalars)
        + [vmem] * len(args)
        + [raw] * len(sources),
        out_specs=tuple(raw if i in raw_out else vmem for i in range(len(outs))),
        scratch_shapes=scratch,
        compiler_params=pltpu.CompilerParams(vmem_limit_bytes=ROOM.get(body, 60) << 20),
        cost_estimate=pl.CostEstimate(
            flops=int(micros * PER_MICRO), bytes_accessed=moved, transcendentals=0
        ),
    )(*scalars, *args, *sources)


def held(count):
    return [VM((count, D, D), LOW), DMA((2 * count,))]


def terms(count):
    return [VM((count, D, D), LOW), DMA((2 * count,))]


def corner_terms(keep, got, half_a, half_b):
    total = keep[...].astype(F32) + got[...].astype(F32)
    half_a[...] = total[:, :PART].astype(LOW)
    half_b[...] = total[:, PART:].astype(LOW)


def side_terms(keep_x, got_x, keep_y, got_y, half_a, half_b, *outs):
    count = len(outs) // 2
    for n in range(count):
        over_x, over_y = outs[n], outs[count + n]
        total = keep_x[n].astype(F32) + got_x[0, n].astype(F32)
        over_x[0, :PART] = (total[:PART] + half_a[n].astype(F32)).astype(LOW)
        over_x[0, PART:] = total[PART:].astype(LOW)
        total = keep_y[n].astype(F32) + got_y[0, n].astype(F32)
        over_y[0, :PART] = total[:PART].astype(LOW)
        over_y[0, PART:] = (total[PART:] + half_b[n].astype(F32)).astype(LOW)


def own_terms(keep, got, from_x, from_y, total, low):
    value = keep[0].astype(F32) + got[0, 0].astype(F32)
    value = value + from_x[0].astype(F32) + from_y[0].astype(F32)
    total[0] = value
    low[0] = value.astype(LOW)


SPLIT = 2


def call_small(body, args, picks, shapes):
    count = args[0].shape[0]
    width = D // SPLIT
    specs = []
    for arg, pick in zip(args, picks):
        if pick is None:
            specs.append(pl.BlockSpec((*arg.shape[:-1], width), lambda j: (0, 0, j)))
        elif isinstance(pick, tuple) and pick[0] == "keep":
            specs.append(pl.BlockSpec((1, SPAN, width), lambda j, k=pick[1]: (k, 0, j)))
        elif isinstance(pick, tuple):
            specs.append(
                pl.BlockSpec((1, 1, SPAN, width), lambda j, k=pick[1]: (0, k, 0, j))
            )
        elif isinstance(pick, int):
            specs.append(
                pl.BlockSpec((1, count, SPAN, width), lambda j, k=pick: (k, 0, 0, j))
            )
    moved = sum(s.block_shape[-2] * D * count * 2 for s in specs)
    return pl.pallas_call(
        body,
        name=body.__name__,
        grid=(SPLIT,),
        out_shape=tuple(
            jax.ShapeDtypeStruct((*shape, D), dtype) for shape, dtype in shapes
        ),
        in_specs=specs,
        out_specs=tuple(
            pl.BlockSpec((*shape, width), lambda j: (0, 0, j)) for shape, _d in shapes
        ),
        compiler_params=pltpu.CompilerParams(vmem_limit_bytes=24 << 20),
        cost_estimate=pl.CostEstimate(
            flops=int(8 * PER_MICRO), bytes_accessed=moved, transcendentals=0
        ),
    )(*args)


def swap_pairs(count, bit):
    return [(i, i ^ bit) for i in range(count)]


def after(value, *before):
    return lax.optimization_barrier((value, *before))[0]


def add(*parts):
    total = parts[0].astype(F32)
    for part in parts[1:]:
        total = total + part.astype(F32)
    return total


def together(*values):
    return lax.optimization_barrier(values)


class Staged:
    planes = 4
    tables = ((0, 1, 2, 2), (1, 0, 1, 3), (2, 2, 0, 1), (3, 3, 3, 0))

    def __init__(self):
        self.count = NMAT
        self.step = NMAT // self.planes
        cols = lax.axis_index("cols")
        self.z = cols // self.step
        self.place = jnp.stack(
            [lax.axis_index("fsdp"), (cols // 2) % 2, cols % 2, self.z]
        ).astype(jnp.int32)

    def over_x(self, value):
        return lax.ppermute(value, "fsdp", [(0, 1), (1, 0)])

    def over_y(self, value):
        return lax.ppermute(value, "cols", swap_pairs(self.count, 2))

    def over_core(self, value):
        return lax.ppermute(value, "cols", swap_pairs(self.count, 1))

    def over_z(self, value, pairs):
        step = self.step
        full = [(a * step + i, b * step + i) for a, b in pairs for i in range(step)]
        return lax.ppermute(value, "cols", full)

    def by_plane(self, options):
        result = options[-1]
        for index in range(len(options) - 2, -1, -1):
            result = jnp.where(self.z == index, options[index], result)
        return result

    def own_place(self, gains):
        index = lax.axis_index("cols") * 2 + lax.axis_index("fsdp")
        spread = jnp.zeros((EXTRA * D,), LOW)
        spread = lax.dynamic_update_slice(spread, gains, (index * gains.shape[0],))
        return spread.reshape(EXTRA, D)

    def sum_step(self, value, index):
        swaps = (
            self.over_core,
            self.over_x,
            self.over_y,
            lambda v: self.over_z(v, [(0, 1), (1, 0), (2, 3), (3, 2)]),
            lambda v: self.over_z(v, [(0, 2), (2, 0), (1, 3), (3, 1)]),
        )
        return value + swaps[index](value)

    def own_gains(self, value, size):
        value = value.reshape(3 * D)
        index = lax.axis_index("cols") * 2 + lax.axis_index("fsdp")
        return lax.dynamic_slice(value, (index * size,), (size,))

    def halves(self, from_x, from_y):
        return self.over_y(from_x[:PART]), self.over_x(from_y[PART:])

    def gather(self, shard, gains, tokens):
        core = self.over_core
        own1 = jnp.concatenate([shard, self.own_place(gains)], axis=0)
        up1 = self.over_z(own1, [(0, 1), (1, 2), (2, 3)])
        down1 = self.over_z(own1, [(3, 2), (2, 1), (1, 0)])
        x1, y1 = self.over_x(own1), self.over_y(own1)
        up1, down1, x1, y1 = together(up1, down1, x1, y1)
        own2 = jnp.where(self.z == 0, down1, up1)
        x2, y2 = self.over_x(own2), self.over_y(own2)
        a1, b1 = self.halves(x1, y1)
        up2 = self.over_z(up1, [(1, 2), (2, 3)])
        down2 = self.over_z(down1, [(2, 1), (1, 0)])
        rims = neighbours(*after((tokens[:, CB - HALO :], tokens[:, :HALO]), x1))
        c1 = [core(own1)]
        up2, down2, a1, b1, x2, y2, *rims = together(up2, down2, a1, b1, x2, y2, *rims)
        up3 = self.over_z(up2, [(2, 3)])
        down3 = self.over_z(down2, [(1, 0)])
        a2, b2 = self.halves(x2, y2)
        c1 += [core(x1), core(y1), core(a1), core(b1)]
        up3, down3, a2, b2, *c1 = together(up3, down3, a2, b2, *c1)
        own3 = self.by_plane([down2, down1, up2, up3])
        placed = [v[SPAN:] for v in (own1, up1, up2, up3, down1, down2, down3)]
        own3 = jnp.concatenate([own3[:SPAN], add(*placed).astype(LOW)], axis=0)
        x3, y3 = self.over_x(own3), self.over_y(own3)
        c2 = [core(v) for v in (own2, x2, y2, a2, b2)]
        x3, y3, *c2 = together(x3, y3, *c2)
        a3, b3 = self.halves(x3, y3)
        c3 = [core(own3), core(x3), core(y3)]
        own4 = self.by_plane([down3, down2, down1, up2])
        a3, b3, own4, *c3 = together(a3, b3, own4, *c3)
        x4, y4 = self.over_x(own4), self.over_y(own4)
        c3 += [core(a3), core(b3)]
        self.row_gate = (own4,)
        self.fourth = own4, x4, y4
        self.first = ((own1, x1, y1, a1, b1), tuple(c1), (own2, x2, y2, a2, b2), tuple(c2))
        self.first += ((own3, x3, y3, a3, b3), tuple(c3))
        return (self.tables[0], self.first), 2, rims

    def gather_more(self, seen):
        own4, x4, y4 = self.fourth
        x4, y4, seen = together(x4, y4, seen)
        xa, yb = x4[:PART], y4[PART:]
        self.attend_gate = (xa, yb)
        core = self.over_core
        self.fourth = own4, x4, y4, self.over_y(xa), self.over_x(yb)
        self.fourth_core = [core(own4), core(x4), core(y4)]

    def gather_last(self, seen):
        own4, x4, y4, a4, b4 = self.fourth
        a4, b4, _ = together(a4, b4, seen)
        core = self.over_core
        c4 = (*self.fourth_core, core(a4), core(b4))
        every = (*self.first, (own4, x4, y4, a4, b4), c4)
        return (self.tables[1], every), (self.tables[2:], every)

    def corner_swap(self, keep, got):
        shapes = (((keep[3].shape[0], PART), LOW),) * 2
        return call_small(corner_terms, (keep[3], got), (None, None), shapes)

    def side_blocks(self, keep, got, corner_a, corner_b):
        picks = (None, 1, None, 2, None, None)
        args = (keep[1], got, keep[2], got, corner_a, corner_b)
        count = keep[0].shape[0]
        sides = call_small(side_terms, args, picks, (((1, SPAN), LOW),) * (2 * count))
        return sides[:count], sides[count:]

    def own_sum(self, keep, got, from_x, from_y, n=0):
        shapes = (((1, SPAN), F32), ((1, SPAN), LOW))
        picks = (("keep", n), ("got", n), None, None)
        total, low = call_small(own_terms, (keep[0], got, from_x, from_y), picks, shapes)
        return total[0], low[0]

    def reduce_forward(self, *terms):
        *keep, rest, corner = terms
        corner = self.over_core(corner)
        a, b = self.corner_swap(keep, corner)
        self.fwd = keep, self.over_core(after(rest, a, b))
        self.fwd_corner = self.over_y(a), self.over_x(b)
        return a, b

    def reduce_forward_sides(self, seen):
        a, b, _ = together(*self.fwd_corner, seen)
        (x2, x3), (y2, y3) = self.side_blocks(*self.fwd, a, b)
        self.first_sides = self.over_x(x2), self.over_y(y2)
        self.later_sides = x3, y3
        return x2, y2, x3, y3

    def reduce_col(self, *terms):
        *keep, rest, corner = terms
        corner = self.over_core(corner)
        fx, fy = together(*self.first_sides)
        a, b = after(self.later_sides, fx, fy)
        self.later_sides = self.over_x(a), self.over_y(b)
        a, b = self.corner_swap(keep, after(corner, a, b))
        self.col = keep, self.over_core(after(rest, a, b))
        self.col_corner = self.over_y(a), self.over_x(b)
        fx, fy, *_ = together(fx, fy, a, b)
        self.second, low = self.own_sum(*self.fwd, fx, fy, 0)
        self.near_second = self.over_z(low, [(0, 1), (3, 2)])
        return a, b, low

    def reduce_row(self, seen, *terms):
        *keep, rest, corner = terms
        corner = self.over_core(corner)
        a, b, fx, fy, near, _ = together(
            *self.col_corner, *self.later_sides, self.near_second, seen
        )
        (cx,), (cy,) = self.side_blocks(*self.col, a, b)
        corner = after(corner, cx, cy)
        cx, cy = self.over_x(cx), self.over_y(cy)
        a, b = self.corner_swap(keep, corner)
        got = self.over_core(after(rest, a, b))
        fx, fy, near, *_ = together(fx, fy, near, a, b)
        a, b = self.over_y(a), self.over_x(b)
        self.third, low = self.own_sum(*self.fwd, fx, fy, 1)
        self.near_third = self.over_z(low, [(0, 1), (2, 3)])
        self.second = add(self.second, near)
        second_low = self.second.astype(LOW)
        self.far_second = self.over_z(second_low, [(1, 2)])
        a, b, cx, cy, got, *_ = together(a, b, cx, cy, got, low, second_low)
        (rx,), (ry,) = self.side_blocks(keep, got, a, b)
        cx, cy, *_ = together(cx, cy, rx, ry)
        self.row = keep, got
        self.row_sides = self.over_x(rx), self.over_y(ry)
        self.col_sum, low = self.own_sum(*self.col, cx, cy)
        self.near_col = self.over_z(low, [(0, 1), (3, 2)])
        return rx, ry, low

    def reduce_last(self, gains):
        rx, ry, near_col, near, far_second, gains = together(
            *self.row_sides, self.near_col, self.near_third, self.far_second, gains
        )
        row, low = self.own_sum(*self.row, rx, ry)
        near_row = self.over_z(low, [(1, 0), (3, 2)])
        self.rim_gate = (low,)
        near_col, near, gains, _ = together(near_col, near, gains, low)
        col = add(self.col_sum, near_col)
        far_col = self.over_z(col.astype(LOW), [(2, 1)])
        third = add(self.third, near)
        far_third = self.over_z(third.astype(LOW), [(1, 3)])
        gains = gains.reshape(18, LANES)
        for index in range(4):
            gains = self.sum_step(gains, index)
        near_row, far_col, far_third, gains = together(near_row, far_col, far_third, gains)
        row = add(row, near_row)
        low = row.astype(LOW)
        far_row = self.over_z(low, [(2, 0)])
        self.last_gate = (low,)
        self.gains = gains
        forward = jnp.where(
            self.z == 2, add(self.second, far_second), add(third, far_third)
        )
        self.totals = row, far_row, jnp.where(self.z == 1, add(col, far_col), forward)

    def total(self, seen):
        row, far_row, rest = self.totals
        far_row, rest, seen, gains = together(far_row, rest, seen, self.gains)
        result = jnp.where(self.z == 0, add(row, far_row), rest)
        return result, seen, self.sum_step(gains, 4)


class Native:
    axes = ("cols", "fsdp")
    rim_gate = ()
    last_gate = ()
    row_gate = ()
    attend_gate = ()

    def __init__(self):
        self.place = jnp.zeros((4,), jnp.int32)
        self.parts = []

    def gather(self, shard, gains, tokens):
        full = lax.all_gather(shard, self.axes, axis=0, tiled=True)
        gains = lax.all_gather(gains, self.axes, axis=0, tiled=True)
        rims = neighbours(tokens[:, CB - HALO :], tokens[:, :HALO])
        row, *self.rest = self.arranged(full, gains)
        return row, 0, rims

    def gather_more(self, seen):
        pass

    def gather_last(self, seen):
        return self.rest

    def arranged(self, full, gains):
        blocks = full.reshape(4, 2, 2, 2 * SPAN, D).transpose(0, 2, 1, 3, 4)
        blocks = blocks.reshape(4, 2, 4, SPAN, D)
        extra = jnp.pad(gains.reshape(3, D), ((0, EXTRA - 3), (0, 0)))
        groups = []
        for b in range(4):
            parts = []
            for c in range(2):
                for k in range(3):
                    mine = extra if b == c == k == 0 else jnp.zeros_like(extra)
                    parts.append(jnp.concatenate([blocks[b, c, k], mine], axis=0))
                last = jnp.concatenate([blocks[b, c, 3], jnp.zeros_like(extra)], axis=0)
                parts += [last[:PART], last[PART:]]
            groups.append((tuple(parts[:5]), tuple(parts[5:])))
        row, col, low, high = groups
        flat = (0, 0, 0, 0)
        return (flat, row), (flat, col), ((flat, (1, 1, 1, 1)), (*low, *high))

    def own_gains(self, value, size):
        value = value.reshape(3 * D)
        return lax.psum_scatter(value, self.axes, scatter_dimension=0, tiled=True)

    def stash(self, *terms):
        *keep, rest, corner = terms
        sent = jnp.concatenate([rest, corner[None]], axis=0)
        blocks = jnp.stack([jnp.stack(keep), sent])
        blocks = blocks.reshape(2, 2, 2, *corner.shape)
        self.parts.insert(0, blocks.transpose(3, 1, 0, 2, 4, 5))
        return ()

    def reduce_forward(self, *terms):
        return self.stash(*terms)

    def reduce_forward_sides(self, seen):
        return ()

    def reduce_col(self, *terms):
        return self.stash(*terms)

    def reduce_row(self, seen, *terms):
        return self.stash(*terms)

    def reduce_last(self, gains):
        self.gains = gains

    def total(self, seen):
        full = jnp.concatenate([self.parts[0], self.parts[1], self.parts[2]], axis=0)
        full = full.reshape(NMAT * D, D)
        full = lax.psum_scatter(full, self.axes, scatter_dimension=0, tiled=True)
        return full.astype(F32), seen, self.gains


def neighbours(upward, downward):
    count = lax.axis_size("cols")
    forward = [(i, i + 1) for i in range(count - 1)]
    backward = [(target, source) for source, target in forward]
    return lax.ppermute(upward, "cols", forward), lax.ppermute(downward, "cols", backward)


def adamw(master, moment, square, grad_total, rate, decay, steps_done):
    moment_new = BETA_ONE * moment + (1.0 - BETA_ONE) * grad_total
    square_new = BETA_TWO * square + (1.0 - BETA_TWO) * grad_total * grad_total
    moment_fix = 1.0 - BETA_ONE**steps_done
    square_fix = 1.0 - BETA_TWO**steps_done
    update = moment_new / moment_fix / (jnp.sqrt(square_new / square_fix) + ADAM_EPS)
    return (master - rate * (update + decay * master), moment_new, square_new)


def band_mask(band_reach):
    first_col = lax.axis_index("cols") * CB
    col_total = CB * lax.axis_size("cols")
    query_pos = first_col + jnp.arange(CB, dtype=jnp.int32)
    key_pos = first_col - HALO + jnp.arange(EXT, dtype=jnp.int32)
    lowest = query_pos[None] - band_reach[:, 0]
    highest = query_pos[None] + band_reach[:, 1]
    key = key_pos[None, None]
    allowed = (key >= lowest[..., None]) & (key <= highest[..., None])
    allowed = allowed & (key >= 0) & (key < col_total)
    return allowed.astype(F32)


def layer(tokens, cot, counts, reach, mover, shard, gains):
    row_w, group, rims = mover.gather(shard, gains, tokens)
    from_low, from_high = rims
    present = (jnp.arange(ROWS, dtype=jnp.int32)[None] < counts[:, None]).astype(F32)
    row_scale = DH ** (-0.5) * lax.rsqrt(counts.astype(F32))
    scalars = (jnp.concatenate([row_scale[:, None], present], axis=1), mover.place)
    run = partial(run_kernel, scalars=scalars)
    low, wide = (SEQ_CB, LOW), (SEQ_EXT, LOW)
    row_gain = ((1, D), F32)
    probs = ((MB, PAIRS, 2 * CB, EXT), F32)
    col_probs = ((SEQ, ROWS * CB, LANES), F32)

    a1e, q, ke, ve, gain = run(
        row_project,
        args=(after(tokens, *mover.row_gate), from_low, from_high),
        weights=((row_w[0], group), row_w[1]),
        outs=like(wide, low, wide, wide, ((3, D), F32)),
        raw_out=(),
        scratch=[held(3)[0], VM((8, EXTRA, D), LOW), DMA((6,)), DMA((8,))],
        micros=9.5,
    )
    mover.gather_more(q)
    p1, o1, x1, a2 = run(
        row_attend,
        args=(tokens, after(q, *mover.attend_gate), ke, ve, band_mask(reach), gain),
        weights=row_w,
        outs=like(probs, low, (SEQ_CB, F32), low),
        raw_out=(),
        scratch=held(1),
        micros=12.5,
    )
    col_w, forward_w = mover.gather_last(a2)
    q2, k2, v2, p2, o2, x2, a3 = run(
        col_forward,
        args=(x1, a2, gain),
        weights=col_w,
        outs=like(low, low, low, col_probs, low, (SEQ_CB, F32), low),
        raw_out=(),
        scratch=held(4),
        micros=15.5,
    )
    token = (TOK, D)
    out, e2, dg3, *forward_g = run(
        feed_forward,
        args=(x2, a3, cot, gain),
        weights=forward_w,
        outs=like(low, (SEQ_CB, F32), row_gain, *pieces(2)),
        raw_out=range(3, 9),
        scratch=[VM(token, F32)] * 2 + [VM(token, LOW)] * 3 + [held(8)[0], terms(8)[0]]
        + [DMA((16,))] * 2,
        micros=26,
    )
    gate = mover.reduce_forward(*forward_g)
    dq2, dk2, dv2 = run(
        col_attend_back,
        args=(after(e2, *gate), q2, k2, v2, p2),
        weights=col_w,
        outs=like(low, low, low),
        raw_out=(),
        scratch=[VM(SEQ_CB, LOW)] + [VM(SEQ_CB, F32)] * 2 + held(1),
        micros=10.5,
    )
    gate = mover.reduce_forward_sides(dq2)
    dq2 = after(dq2, *gate)
    e1, dg2, *col_g = run(
        col_project_back,
        args=(e2, o2, dq2, dk2, dv2, a2, x1, gain),
        weights=col_w,
        outs=like((SEQ_CB, F32), row_gain, *pieces(1)),
        raw_out=range(2, 8),
        scratch=[VM(SEQ_CB, F32), held(3)[0], terms(4)[0], DMA((6,)), DMA((8,))],
        micros=11.5,
    )
    gate = mover.reduce_col(*col_g)
    dq, dke, dve, *row_g = run(
        row_backward,
        args=(after(e1, *gate), o1, q, ke, ve, p1, a1e),
        weights=row_w,
        outs=like(low, wide, wide, *pieces(1)),
        raw_out=range(3, 9),
        scratch=[VM(SEQ_CB, LOW)] + [held(1)[0], terms(4)[0], DMA((2,)), DMA((8,))],
        micros=20,
    )
    gate = mover.reduce_row(dq, *row_g)
    inner, to_low, to_high, dg1 = run(
        input_project,
        args=(after(dq, *gate), dke, dve, tokens, from_low, from_high),
        weights=row_w,
        outs=like((SEQ_CB, F32), (RIM, LOW), (RIM, LOW), row_gain),
        raw_out=(),
        scratch=[VM(SEQ_EXT, F32)] + held(3),
        micros=8,
    )
    gains = jnp.concatenate([dg1, dg2, dg3], axis=0)
    mover.reduce_last(gains)
    to_high, to_low, *_ = together(to_high, to_low, *mover.rim_gate)
    from_low, from_high = neighbours(to_high, to_low)
    (grad,) = run_kernel(
        input_finish,
        (),
        (after(inner, *mover.last_gate), from_low, from_high, e1, tokens, gain),
        None,
        like(low),
        (),
        (),
        3,
    )
    weight_grad, grad, gains = mover.total(grad)
    return out, grad, weight_grad, gains


def per_device(
    alignment,
    cotangent,
    row_counts,
    band_reach,
    master_weights,
    weight_moment,
    weight_square,
    norm_gains,
    gain_moment,
    gain_square,
):
    staged = lax.axis_size("cols") == NMAT and lax.axis_size("fsdp") == 2
    mover = Staged() if staged else Native()
    out, grad, weight_total, gain_grad = layer(
        alignment.reshape(SEQ, CB, D),
        cotangent.reshape(SEQ, CB, D),
        row_counts[:, 0],
        band_reach[:, 0],
        mover,
        master_weights.astype(LOW),
        norm_gains.astype(LOW),
    )
    gain_total = mover.own_gains(gain_grad, norm_gains.shape[0])
    new_weights, new_moment, new_square = adamw(
        master_weights,
        weight_moment,
        weight_square,
        weight_total.reshape(master_weights.shape),
        D ** (-0.5),
        DECAY,
        STEP_NUMBER,
    )
    new_gains, new_gain_moment, new_gain_square = adamw(
        norm_gains, gain_moment, gain_square, gain_total, RATE_GAIN, 0.0, STEP_NUMBER
    )
    shape = (MB, 1, ROWS, CB, D)
    return (
        out.reshape(shape),
        grad.reshape(shape),
        new_weights,
        new_moment,
        new_square,
        new_weights.astype(LOW),
        new_gains,
        new_gain_moment,
        new_gain_square,
    )


def solution(mesh):
    tokens = P(None, "fsdp", None, "cols", None)
    rows = P(("cols", "fsdp"), None)
    flat = P(("cols", "fsdp"))
    in_specs = (
        tokens,
        tokens,
        P(None, "fsdp"),
        P(None, "fsdp", None, "cols"),
        rows,
        rows,
        rows,
        flat,
        flat,
        flat,
    )
    out_specs = (tokens, tokens, rows, rows, rows, rows, flat, flat, flat)
    return jax.shard_map(
        per_device, mesh=mesh, in_specs=in_specs, out_specs=out_specs, check_vma=False
    )
```

profile of v0, /device:TPU:0, one launch (start us, length us, event | category | flops | bytes accessed | tf_op | source)
XLA Modules:
  0.0 356.0 jit_solution(5875530265971693995)
XLA Ops:
  3.0 3.0 collective-permute-start.3
  8.8 5.4 %collective-permute-start = (bf16[400,768]{1,0:T(8,128)(2,1)S(1)}, bf16[400,768]{1,0:T(8,128)(2,1)}, u32[]{:S(2)}, u32[]{:S(2)}) collective-permute-start(bf16[400,768]{1,0:T(8,128)(2,1)S(1)} %pad_maximum_fusion.refs_0_), channel_id=1, source_target_pairs={{0,8},{2,10},{4,12},{6,14},{8,16},{10,18},{12,20},{14,22},{16,24},... | collective-permute-start | bytes 1843208 | tf_op jit(solution)/shard_map/ppermute | solution.py:700
  14.1 5.7 %collective-permute-done.3.refs_2_ = bf16[400,768]{1,0:T(8,128)(2,1)S(1)} collective-permute-done((bf16[400,768]{1,0:T(8,128)(2,1)S(1)}, bf16[400,768]{1,0:T(8,128)(2,1)S(1)}, u32[]{:S(2)}, u32[]{:S(2)}) %collective-permute-start.3) | collective-permute-done | bytes 614432 | tf_op jit(solution)/shard_map/ppermute | solution.py:692
  21.3 3.1 collective-permute-done.1
  30.5 4.7 %collective-permute-start.9 = (bf16[400,768]{1,0:T(8,128)(2,1)S(1)}, bf16[400,768]{1,0:T(8,128)(2,1)S(1)}, u32[]{:S(2)}, u32[]{:S(2)}) collective-permute-start(bf16[400,768]{1,0:T(8,128)(2,1)S(1)} %broadcast_select_fusion.refs_10_), channel_id=1, source_target_pairs={{0,4},{2,6},{4,0},{6,2},{8,12},{10,14},{12,8},{14,10},{16,20},{18,... | collective-permute-start | bytes 1843208 | tf_op jit(solution)/shard_map/ppermute | solution.py:692
  39.5 5.7 %collective-permute-start.16 = (bf16[400,768]{1,0:T(8,128)(2,1)S(1)}, bf16[400,768]{1,0:T(8,128)(2,1)S(1)}, u32[]{:S(2)}, u32[]{:S(2)}) collective-permute-start(bf16[400,768]{1,0:T(8,128)(2,1)S(1)} %pad_maximum_fusion.refs_0_), channel_id=1, source_target_pairs={{0,2},{2,0},{4,6},{6,4},{8,10},{10,8},{12,14},{14,12},{16,18},{18,... | collective-permute-start | bytes 1843208 | tf_op jit(solution)/shard_map/ppermute | solution.py:695
  45.2 8.9 %collective-permute-done.9.refs_12_ = bf16[400,768]{1,0:T(8,128)(2,1)S(1)} collective-permute-done((bf16[400,768]{1,0:T(8,128)(2,1)S(1)}, bf16[400,768]{1,0:T(8,128)(2,1)S(1)}, u32[]{:S(2)}, u32[]{:S(2)}) %collective-permute-start.9) | collective-permute-done | bytes 614432 | tf_op jit(solution)/shard_map/ppermute | solution.py:692
  54.7 5.3 %collective-permute-done.5 = bf16[400,768]{1,0:T(8,128)(2,1)} collective-permute-done((bf16[400,768]{1,0:T(8,128)(2,1)}, bf16[400,768]{1,0:T(8,128)(2,1)}, u32[]{:S(2)}, u32[]{:S(2)}) %collective-permute-start.5) | collective-permute-done | bytes 614432 | tf_op jit(solution)/shard_map/ppermute | solution.py:700
  65.4 5.3 %collective-permute-done.14.refs_13_ = bf16[192,768]{1,0:T(8,128)(2,1)S(1)} collective-permute-done((bf16[192,768]{1,0:T(8,128)(2,1)S(1)}, bf16[192,768]{1,0:T(8,128)(2,1)S(1)}, u32[]{:S(2)}, u32[]{:S(2)}) %collective-permute-start.14) | collective-permute-done | bytes 294944 | tf_op jit(solution)/shard_map/ppermute | solution.py:692
  73.2 3.1 collective-permute-done.13
  82.7 9.7 %collective-permute-done.22.refs_22_ = bf16[400,768]{1,0:T(8,128)(2,1)S(1)} collective-permute-done((bf16[400,768]{1,0:T(8,128)(2,1)S(1)}, bf16[400,768]{1,0:T(8,128)(2,1)S(1)}, u32[]{:S(2)}, u32[]{:S(2)}) %collective-permute-start.22) | collective-permute-done | bytes 614432 | tf_op jit(solution)/shard_map/ppermute | solution.py:692
  99.4 5.1 %collective-permute-done.28.refs_23_ = bf16[192,768]{1,0:T(8,128)(2,1)S(1)} collective-permute-done((bf16[192,768]{1,0:T(8,128)(2,1)S(1)}, bf16[192,768]{1,0:T(8,128)(2,1)S(1)}, u32[]{:S(2)}, u32[]{:S(2)}) %collective-permute-start.28) | collective-permute-done | bytes 294944 | tf_op jit(solution)/shard_map/ppermute | solution.py:692
  110.7 10.7 %row_project.1 = (bf16[8,128,768]{2,1,0:T(8,128)(2,1)}, bf16[8,64,768]{2,1,0:T(8,128)(2,1)}, bf16[8,128,768]{2,1,0:T(8,128)(2,1)}, bf16[8,128,768]{2,1,0:T(8,128)(2,1)}, f32[3,768]{1,0:T(4,128)}) custom-call(f32[2,5]{1,0:T(2,128)} %pad_maximum_fusion.3.scal, s32[4]{0:T(128)} %pad_add_fusion.place, bf16[8,64,768]{2,1,0:T(8,128)(2,1)} %bitcast.46, ...), custom_call_target="tpu_custom_call" | custom-call | flops 10924999680 | bytes 7087104 | tf_op jit(solution)/shard_map/row_project/pallas_call | solution.py:568
  126.8 7.5 %row_attend.1 = (f32[2,6,128,128]{3,2,1,0:T(8,128)}, bf16[8,64,768]{2,1,0:T(8,128)(2,1)}, f32[8,64,768]{2,1,0:T(8,128)}, bf16[8,64,768]{2,1,0:T(8,128)(2,1)}) custom-call(f32[2,5]{1,0:T(2,128)} %pad_maximum_fusion.3.scal, s32[4]{0:T(128)} %pad_add_fusion.place, bf16[8,64,768]{2,1,0:T(8,128)(2,1)} %bitcast.47, bf16[8,64,768]{2,1,0:T(8,128)(2,1)} %get-tuple-element.214.q, ...), custom_call_target="tpu_custom_call" | custom-call | flops 14375000064 | bytes 8725504 | tf_op jit(solution)/shard_map/row_attend/pallas_call | solution.py:568
  137.3 11.9 %col_forward.1 = (bf16[8,64,768]{2,1,0:T(8,128)(2,1)}, bf16[8,64,768]{2,1,0:T(8,128)(2,1)}, bf16[8,64,768]{2,1,0:T(8,128)(2,1)}, f32[8,256,128]{2,1,0:T(8,128)},...) custom-call(f32[2,5]{1,0:T(2,128)} %pad_maximum_fusion.3.scal, ...), custom_call_target="tpu_custom_call" | custom-call | flops 17824999424 | bytes 8922112 | tf_op jit(solution)/shard_map/col_forward/pallas_call | solution.py:568
  149.1 23.1 %feed_forward.1 = (bf16[8,64,768]{2,1,0:T(8,128)(2,1)}, f32[8,64,768]{2,1,0:T(8,128)}, f32[1,768]{1,0:T(1,128)}, bf16[2,384,768]{2,1,0:T(8,128)(2,1)}, bf16[2,38...) custom-call(f32[2,5]{1,0:T(2,128)} %pad_maximum_fusion.3.scal, ...), custom_call_target="tpu_custom_call" | custom-call | flops 29899999232 | bytes 14954496 | tf_op jit(solution)/shard_map/feed_forward/pallas_call | solution.py:568
  172.5 2.9 collective-permute-done.44.got
  180.8 9.4 %col_attend_back.1 = (bf16[8,64,768]{2,1,0:T(8,128)(2,1)}, bf16[8,64,768]{2,1,0:T(8,128)(2,1)}, bf16[8,64,768]{2,1,0:T(8,128)(2,1)}) custom-call(f32[2,5]{1,0:T(2,128)S(1)} %copy-done.23, s32[4]{0:T(128)S(1)} %copy-done.24, f32[8,64,768]{2,1,0:T(8,128)} %get-tuple-element.231.e2, bf16[8,64,768]{2,1,0:T(8,128)(2,1)} %get-tuple-element.232.q2, ...), custom_call_target="tpu_custom_call" | custom-call | flops 12074999808 | bytes 7340032 | tf_op jit(solution)/shard_map/col_attend_back/pallas_call | solution.py:568
  190.3 3.1 collective-permute-done.46.half_a
  197.5 12.7 %col_project_back.1 = (f32[8,64,768]{2,1,0:T(8,128)}, f32[1,768]{1,0:T(1,128)S(1)}, bf16[1,384,768]{2,1,0:T(8,128)(2,1)S(1)}, bf16[1,384,768]{2,1,0:T(8,128)(2,1...) custom-call(f32[2,5]{1,0:T(2,128)S(1)} %copy-done.23, ...), custom_call_target="tpu_custom_call" | custom-call | flops 13224999936 | bytes 13381632 | tf_op jit(solution)/shard_map/col_project_back/pallas_call | solution.py:568
  217.7 6.0 %collective-permute-start.57 = (bf16[384,768]{1,0:T(8,128)(2,1)S(1)}, bf16[384,768]{1,0:T(8,128)(2,1)}, u32[]{:S(2)}, u32[]{:S(2)}) collective-permute-start(bf16[384,768]{1,0:T(8,128)(2,1)S(1)} %bitcast.53), channel_id=1, source_target_pairs={{0,8},{2,10},{4,12},{6,14},{24,16},{26,18},{28,20},{30,22},{1,9},{... | collective-permute-start | bytes 1769480 | tf_op jit(solution)/shard_map/ppermute | solution.py:700
  223.7 18.9 %row_backward.1 = (bf16[8,64,768]{2,1,0:T(8,128)(2,1)}, bf16[8,128,768]{2,1,0:T(8,128)(2,1)}, bf16[8,128,768]{2,1,0:T(8,128)(2,1)}, bf16[1,384,768]{2,1,0:T(8,12...) custom-call(f32[2,5]{1,0:T(2,128)S(1)} %copy-done.23, ...), custom_call_target="tpu_custom_call" | custom-call | flops 23000000512 | bytes 17301504 | tf_op jit(solution)/shard_map/row_backward/pallas_call | solution.py:568
  255.3 2.9 collective-permute-done.58.half_a
  259.6 9.1 %collective-permute-start.66 = (bf16[384,768]{1,0:T(8,128)(2,1)S(1)}, bf16[384,768]{1,0:T(8,128)(2,1)}, u32[]{:S(2)}, u32[]{:S(2)}) collective-permute-start(bf16[384,768]{1,0:T(8,128)(2,1)S(1)} %bitcast.51), channel_id=1, source_target_pairs={{0,8},{2,10},{4,12},{6,14},{16,24},{18,26},{20,28},{22,30},{1,9},{... | collective-permute-start | bytes 1769480 | tf_op jit(solution)/shard_map/ppermute | solution.py:700
  273.5 5.1 %collective-permute-start.65 = (bf16[384,768]{1,0:T(8,128)(2,1)S(1)}, bf16[384,768]{1,0:T(8,128)(2,1)S(1)}, u32[]{:S(2)}, u32[]{:S(2)}) collective-permute-start(bf16[384,768]{1,0:T(8,128)(2,1)S(1)} %bitcast.52), channel_id=1, source_target_pairs={{0,8},{2,10},{4,12},{6,14},{24,16},{26,18},{28,20},{30,22},{1,9},{... | collective-permute-start | bytes 1769480 | tf_op jit(solution)/shard_map/ppermute | solution.py:700
  281.0 10.5 %input_project.1 = (f32[8,64,768]{2,1,0:T(8,128)}, bf16[8,32,768]{2,1,0:T(8,128)(2,1)S(1)}, bf16[8,32,768]{2,1,0:T(8,128)(2,1)S(1)}, f32[1,768]{1,0:T(1,128)S(1)}) custom-call(f32[2,5]{1,0:T(2,128)S(1)} %copy-done.23, s32[4]{0:T(128)S(1)} %copy-done.24, bf16[8,64,768]{2,1,0:T(8,128)(2,1)} %get-tuple-element.306.dq, ...), custom_call_target="tpu_custom_call" | custom-call | flops 9200000000 | bytes 7867392 | tf_op jit(solution)/shard_map/input_project/pallas_call | solution.py:568
  306.8 3.1 collective-permute-done.72
  310.7 2.9 collective-permute-done.73
  314.2 4.8 %collective-permute-start.74 = (f32[18,128]{1,0:T(8,128)S(1)}, f32[18,128]{1,0:T(8,128)S(1)}, u32[]{:S(2)}, u32[]{:S(2)}) collective-permute-start(f32[18,128]{1,0:T(8,128)S(1)} %add.163), channel_id=1, source_target_pairs={{0,8},{2,10},{4,12},{6,14},{8,0},{10,2},{12,4},{14,6},{16,24},{18,... | collective-permute-start | bytes 27656 | tf_op jit(solution)/shard_map/ppermute | solution.py:700
  328.2 3.1 input_finish.1
  333.9 16.7 %collective-permute-done.75 = bf16[384,768]{1,0:T(8,128)(2,1)S(1)} collective-permute-done((bf16[384,768]{1,0:T(8,128)(2,1)S(1)}, bf16[384,768]{1,0:T(8,128)(2,1)S(1)}, u32[]{:S(2)}, u32[]{:S(2)}) %collective-permute-start.75) | collective-permute-done | bytes 589856 | tf_op jit(solution)/shard_map/ppermute | solution.py:700
  350.6 3.9 %fusion.7 = (bf16[384,768]{1,0:T(8,128)(2,1)}, f32[384,768]{1,0:T(8,128)}, f32[384,768]{1,0:T(8,128)}, f32[384,768]{1,0:T(8,128)}) fusion(f32[384,768]{1,0:T(8,128)S(1)} %copy-done.102, f32[384,768]{1,0:T(8,128)S(1)} %copy-done.105, f32[384,768]{1,0:T(8,128)S(1)} %copy-done.106, f32[384,768]{1,0:T(8,128)S(1)} %select_select_fusion, ...), kind=kLoop, calls=%fused_computation.39 | loop fusion | flops 6193152 | bytes 11206657 | tf_op jit(solution)/shard_map/convert_element_type | solution.py:1152
  (428 shorter events, 120.3 us)
Async XLA Ops:
  3.0 16.9 %collective-permute-start.3 = (bf16[400,768]{1,0:T(8,128)(2,1)S(1)}, bf16[400,768]{1,0:T(8,128)(2,1)S(1)}, u32[]{:S(2)}, u32[]{:S(2)}) collective-permute-start(bf16[400,768]{1,0:T(8,128)(2,1)S(1)} %pad_maximum_fusion.refs_0_), channel_id=1, source_target_pairs={{0,4},{2,6},{4,0},{6,2},{8,12},{10,14},{12,8},{14,10},{16,20},{18,... | collective-permute-start | bytes 1843208 | tf_op jit(solution)/shard_map/ppermute | solution.py:692
  6.0 15.3 %collective-permute-start.2 = (bf16[400,768]{1,0:T(8,128)(2,1)S(1)}, bf16[400,768]{1,0:T(8,128)(2,1)S(1)}, u32[]{:S(2)}, u32[]{:S(2)}) collective-permute-start(bf16[400,768]{1,0:T(8,128)(2,1)S(1)} %pad_maximum_fusion.refs_0_), channel_id=1, source_target_pairs={{0,1},{1,0},{2,3},{3,2},{4,5},{5,4},{6,7},{7,6},{8,9},{9,8},{10,11... | collective-permute-start | bytes 1843208 | tf_op jit(solution)/shard_map/ppermute | solution.py:689
  7.5 16.9 %collective-permute-start.1 = (bf16[400,768]{1,0:T(8,128)(2,1)S(1)}, bf16[400,768]{1,0:T(8,128)(2,1)S(1)}, u32[]{:S(2)}, u32[]{:S(2)}) collective-permute-start(bf16[400,768]{1,0:T(8,128)(2,1)S(1)} %pad_maximum_fusion.refs_0_), channel_id=1, source_target_pairs={{24,16},{26,18},{28,20},{30,22},{16,8},{18,10},{20,12},{22,14},{8,... | collective-permute-start | bytes 1843208 | tf_op jit(solution)/shard_map/ppermute | solution.py:700
  8.8 16.8 %collective-permute-start = (bf16[400,768]{1,0:T(8,128)(2,1)S(1)}, bf16[400,768]{1,0:T(8,128)(2,1)}, u32[]{:S(2)}, u32[]{:S(2)}) collective-permute-start(bf16[400,768]{1,0:T(8,128)(2,1)S(1)} %pad_maximum_fusion.refs_0_), channel_id=1, source_target_pairs={{0,8},{2,10},{4,12},{6,14},{8,16},{10,18},{12,20},{14,22},{16,24},... | collective-permute-start | bytes 1843208 | tf_op jit(solution)/shard_map/ppermute | solution.py:700
  30.5 23.6 %collective-permute-start.9 = (bf16[400,768]{1,0:T(8,128)(2,1)S(1)}, bf16[400,768]{1,0:T(8,128)(2,1)S(1)}, u32[]{:S(2)}, u32[]{:S(2)}) collective-permute-start(bf16[400,768]{1,0:T(8,128)(2,1)S(1)} %broadcast_select_fusion.refs_10_), channel_id=1, source_target_pairs={{0,4},{2,6},{4,0},{6,2},{8,12},{10,14},{12,8},{14,10},{16,20},{18,... | collective-permute-start | bytes 1843208 | tf_op jit(solution)/shard_map/ppermute | solution.py:692
  35.2 18.9 %collective-permute-start.8 = (bf16[400,768]{1,0:T(8,128)(2,1)S(1)}, bf16[400,768]{1,0:T(8,128)(2,1)S(1)}, u32[]{:S(2)}, u32[]{:S(2)}) collective-permute-start(bf16[400,768]{1,0:T(8,128)(2,1)S(1)} %broadcast_select_fusion.refs_10_), channel_id=1, source_target_pairs={{0,1},{1,0},{2,3},{3,2},{4,5},{5,4},{6,7},{7,6},{8,9},{9,8},{10,11... | collective-permute-start | bytes 1843208 | tf_op jit(solution)/shard_map/ppermute | solution.py:689
  36.6 18.0 %collective-permute-start.4 = (bf16[400,768]{1,0:T(8,128)(2,1)}, bf16[400,768]{1,0:T(8,128)(2,1)}, u32[]{:S(2)}, u32[]{:S(2)}) collective-permute-start(bf16[400,768]{1,0:T(8,128)(2,1)} %collective-permute-done), channel_id=1, source_target_pairs={{8,16},{10,18},{12,20},{14,22},{16,24},{18,26},{20,28},{22,30},{9,... | collective-permute-start | bytes 1843208 | tf_op jit(solution)/shard_map/ppermute | solution.py:700
  38.1 21.8 %collective-permute-start.5 = (bf16[400,768]{1,0:T(8,128)(2,1)}, bf16[400,768]{1,0:T(8,128)(2,1)}, u32[]{:S(2)}, u32[]{:S(2)}) collective-permute-start(bf16[400,768]{1,0:T(8,128)(2,1)} %copy-done.101), channel_id=1, source_target_pairs={{16,8},{18,10},{20,12},{22,14},{8,0},{10,2},{12,4},{14,6},{17,9},{... | collective-permute-start | bytes 1843208 | tf_op jit(solution)/shard_map/ppermute | solution.py:700
  39.5 23.8 %collective-permute-start.16 = (bf16[400,768]{1,0:T(8,128)(2,1)S(1)}, bf16[400,768]{1,0:T(8,128)(2,1)S(1)}, u32[]{:S(2)}, u32[]{:S(2)}) collective-permute-start(bf16[400,768]{1,0:T(8,128)(2,1)S(1)} %pad_maximum_fusion.refs_0_), channel_id=1, source_target_pairs={{0,2},{2,0},{4,6},{6,4},{8,10},{10,8},{12,14},{14,12},{16,18},{18,... | collective-permute-start | bytes 1843208 | tf_op jit(solution)/shard_map/ppermute | solution.py:695
  59.9 16.4 %collective-permute-start.13 = (bf16[400,768]{1,0:T(8,128)(2,1)}, bf16[400,768]{1,0:T(8,128)(2,1)}, u32[]{:S(2)}, u32[]{:S(2)}) collective-permute-start(bf16[400,768]{1,0:T(8,128)(2,1)} %collective-permute-done.5), channel_id=1, source_target_pairs={{8,0},{10,2},{12,4},{14,6},{9,1},{11,3},{13,5},{15,7}} | collective-permute-start | bytes 1843208 | tf_op jit(solution)/shard_map/ppermute | solution.py:700
  81.0 18.3 %collective-permute-start.30 = (bf16[400,768]{1,0:T(8,128)(2,1)S(1)}, bf16[400,768]{1,0:T(8,128)(2,1)}, u32[]{:S(2)}, u32[]{:S(2)}) collective-permute-start(bf16[400,768]{1,0:T(8,128)(2,1)S(1)} %pad_maximum_fusion.1.refs_20_), channel_id=1, source_target_pairs={{0,2},{2,0},{4,6},{6,4},{8,10},{10,8},{12,14},{14,12},{16,18},{18,... | collective-permute-start | bytes 1843208 | tf_op jit(solution)/shard_map/ppermute | solution.py:695
  106.4 28.5 %collective-permute-start.39 = (bf16[400,768]{1,0:T(8,128)(2,1)}, bf16[400,768]{1,0:T(8,128)(2,1)S(1)}, u32[]{:S(2)}, u32[]{:S(2)}) collective-permute-start(bf16[400,768]{1,0:T(8,128)(2,1)} %select_select_fusion.1.refs_30_), channel_id=1, source_target_pairs={{0,2},{2,0},{4,6},{6,4},{8,10},{10,8},{12,14},{14,12},{16,18},{18,... | collective-permute-start | bytes 1843208 | tf_op jit(solution)/shard_map/ppermute | solution.py:695
  106.5 16.4 %collective-permute-start.36 = (bf16[400,768]{1,0:T(8,128)(2,1)}, bf16[400,768]{1,0:T(8,128)(2,1)S(1)}, u32[]{:S(2)}, u32[]{:S(2)}) collective-permute-start(bf16[400,768]{1,0:T(8,128)(2,1)} %select_select_fusion.1.refs_30_), channel_id=1, source_target_pairs={{0,4},{2,6},{4,0},{6,2},{8,12},{10,14},{12,8},{14,10},{16,20},{18,... | collective-permute-start | bytes 1843208 | tf_op jit(solution)/shard_map/ppermute | solution.py:692
  107.8 16.1 %collective-permute-start.35 = (bf16[400,768]{1,0:T(8,128)(2,1)}, bf16[400,768]{1,0:T(8,128)(2,1)S(1)}, u32[]{:S(2)}, u32[]{:S(2)}) collective-permute-start(bf16[400,768]{1,0:T(8,128)(2,1)} %select_select_fusion.1.refs_30_), channel_id=1, source_target_pairs={{0,1},{1,0},{2,3},{3,2},{4,5},{5,4},{6,7},{7,6},{8,9},{9,8},{10,11... | collective-permute-start | bytes 1843208 | tf_op jit(solution)/shard_map/ppermute | solution.py:689
  177.6 16.8 %collective-permute-start.45 = (bf16[3,2,384,768]{3,2,1,0:T(8,128)(2,1)}, bf16[3,2,384,768]{3,2,1,0:T(8,128)(2,1)S(1)}, u32[]{:S(2)}, u32[]{:S(2)}) collective-permute-start(bf16[3,2,384,768]{3,2,1,0:T(8,128)(2,1)} %get-tuple-element.239), channel_id=1, source_target_pairs={{0,2},{2,0},{4,6},{6,4},{8,10},{10,8},{12,14},{14,12},{16,18},{18,... | collective-permute-start | bytes 10616840 | tf_op jit(solution)/shard_map/ppermute | solution.py:695
  177.8 15.6 %collective-permute-start.46 = (bf16[2,192,768]{2,1,0:T(8,128)(2,1)S(1)}, bf16[2,192,768]{2,1,0:T(8,128)(2,1)S(1)}, u32[]{:S(2)}, u32[]{:S(2)}) collective-permute-start(bf16[2,192,768]{2,1,0:T(8,128)(2,1)S(1)} %get-tuple-element.229), channel_id=1, source_target_pairs={{0,4},{2,6},{4,0},{6,2},{8,12},{10,14},{12,8},{14,10},{16,20},{18,... | collective-permute-start | bytes 1769480 | tf_op jit(solution)/shard_map/ppermute | solution.py:692
  179.1 15.3 %collective-permute-start.47 = (bf16[2,192,768]{2,1,0:T(8,128)(2,1)S(1)}, bf16[2,192,768]{2,1,0:T(8,128)(2,1)S(1)}, u32[]{:S(2)}, u32[]{:S(2)}) collective-permute-start(bf16[2,192,768]{2,1,0:T(8,128)(2,1)S(1)} %get-tuple-element.230), channel_id=1, source_target_pairs={{0,1},{1,0},{2,3},{3,2},{4,5},{5,4},{6,7},{7,6},{8,9},{9,8},{10,11... | collective-permute-start | bytes 1769480 | tf_op jit(solution)/shard_map/ppermute | solution.py:689
  214.2 28.5 %collective-permute-start.54 = (bf16[1,192,768]{2,1,0:T(8,128)(2,1)S(1)}, bf16[1,192,768]{2,1,0:T(8,128)(2,1)S(1)}, u32[]{:S(2)}, u32[]{:S(2)}) collective-permute-start(bf16[1,192,768]{2,1,0:T(8,128)(2,1)S(1)} %get-tuple-element.259), channel_id=1, source_target_pairs={{0,1},{1,0},{2,3},{3,2},{4,5},{5,4},{6,7},{7,6},{8,9},{9,8},{10,11... | collective-permute-start | bytes 884744 | tf_op jit(solution)/shard_map/ppermute | solution.py:689
  215.6 27.7 %collective-permute-start.55 = (bf16[1,384,768]{2,1,0:T(8,128)(2,1)S(1)}, bf16[1,384,768]{2,1,0:T(8,128)(2,1)S(1)}, u32[]{:S(2)}, u32[]{:S(2)}) collective-permute-start(bf16[1,384,768]{2,1,0:T(8,128)(2,1)S(1)} %get-tuple-element.255), channel_id=1, source_target_pairs={{0,1},{1,0},{2,3},{3,2},{4,5},{5,4},{6,7},{7,6},{8,9},{9,8},{10,11... | collective-permute-start | bytes 1769480 | tf_op jit(solution)/shard_map/ppermute | solution.py:689
  216.2 27.1 %collective-permute-start.56 = (bf16[1,384,768]{2,1,0:T(8,128)(2,1)S(1)}, bf16[1,384,768]{2,1,0:T(8,128)(2,1)S(1)}, u32[]{:S(2)}, u32[]{:S(2)}) collective-permute-start(bf16[1,384,768]{2,1,0:T(8,128)(2,1)S(1)} %get-tuple-element.256), channel_id=1, source_target_pairs={{0,4},{2,6},{4,0},{6,2},{8,12},{10,14},{12,8},{14,10},{16,20},{18,... | collective-permute-start | bytes 1769480 | tf_op jit(solution)/shard_map/ppermute | solution.py:692
  217.7 25.6 %collective-permute-start.57 = (bf16[384,768]{1,0:T(8,128)(2,1)S(1)}, bf16[384,768]{1,0:T(8,128)(2,1)}, u32[]{:S(2)}, u32[]{:S(2)}) collective-permute-start(bf16[384,768]{1,0:T(8,128)(2,1)S(1)} %bitcast.53), channel_id=1, source_target_pairs={{0,8},{2,10},{4,12},{6,14},{24,16},{26,18},{28,20},{30,22},{1,9},{... | collective-permute-start | bytes 1769480 | tf_op jit(solution)/shard_map/ppermute | solution.py:700
  223.6 19.7 %collective-permute-start.52 = (bf16[3,1,384,768]{3,2,1,0:T(8,128)(2,1)}, bf16[3,1,384,768]{3,2,1,0:T(8,128)(2,1)S(1)}, u32[]{:S(2)}, u32[]{:S(2)}) collective-permute-start(bf16[3,1,384,768]{3,2,1,0:T(8,128)(2,1)} %get-tuple-element.273), channel_id=1, source_target_pairs={{0,2},{2,0},{4,6},{6,4},{8,10},{10,8},{12,14},{14,12},{16,18},{18,... | collective-permute-start | bytes 5308424 | tf_op jit(solution)/shard_map/ppermute | solution.py:695
  248.3 22.7 %collective-permute-start.62 = (bf16[3,1,384,768]{3,2,1,0:T(8,128)(2,1)S(1)}, bf16[3,1,384,768]{3,2,1,0:T(8,128)(2,1)S(1)}, u32[]{:S(2)}, u32[]{:S(2)}) collective-permute-start(bf16[3,1,384,768]{3,2,1,0:T(8,128)(2,1)S(1)} %copy-done.116), channel_id=1, source_target_pairs={{0,2},{2,0},{4,6},{6,4},{8,10},{10,8},{12,14},{14,12},{16,18},{18,... | collective-permute-start | bytes 5308424 | tf_op jit(solution)/shard_map/ppermute | solution.py:695
  251.1 19.9 %collective-permute-start.60 = (bf16[1,384,768]{2,1,0:T(8,128)(2,1)S(1)}, bf16[1,384,768]{2,1,0:T(8,128)(2,1)S(1)}, u32[]{:S(2)}, u32[]{:S(2)}) collective-permute-start(bf16[1,384,768]{2,1,0:T(8,128)(2,1)S(1)} %get-tuple-element.278), channel_id=1, source_target_pairs={{0,1},{1,0},{2,3},{3,2},{4,5},{5,4},{6,7},{7,6},{8,9},{9,8},{10,11... | collective-permute-start | bytes 1769480 | tf_op jit(solution)/shard_map/ppermute | solution.py:689
  251.7 19.3 %collective-permute-start.61 = (bf16[1,384,768]{2,1,0:T(8,128)(2,1)S(1)}, bf16[1,384,768]{2,1,0:T(8,128)(2,1)S(1)}, u32[]{:S(2)}, u32[]{:S(2)}) collective-permute-start(bf16[1,384,768]{2,1,0:T(8,128)(2,1)S(1)} %get-tuple-element.279), channel_id=1, source_target_pairs={{0,4},{2,6},{4,0},{6,2},{8,12},{10,14},{12,8},{14,10},{16,20},{18,... | collective-permute-start | bytes 1769480 | tf_op jit(solution)/shard_map/ppermute | solution.py:692
  258.1 34.0 %collective-permute-start.67 = (bf16[384,768]{1,0:T(8,128)(2,1)}, bf16[384,768]{1,0:T(8,128)(2,1)}, u32[]{:S(2)}, u32[]{:S(2)}) collective-permute-start(bf16[384,768]{1,0:T(8,128)(2,1)} %fusion.1), channel_id=1, source_target_pairs={{8,16},{10,18},{12,20},{14,22},{9,17},{11,19},{13,21},{15,23}} | collective-permute-start | bytes 1769480 | tf_op jit(solution)/shard_map/ppermute | solution.py:700
  259.6 32.5 %collective-permute-start.66 = (bf16[384,768]{1,0:T(8,128)(2,1)S(1)}, bf16[384,768]{1,0:T(8,128)(2,1)}, u32[]{:S(2)}, u32[]{:S(2)}) collective-permute-start(bf16[384,768]{1,0:T(8,128)(2,1)S(1)} %bitcast.51), channel_id=1, source_target_pairs={{0,8},{2,10},{4,12},{6,14},{16,24},{18,26},{20,28},{22,30},{1,9},{... | collective-permute-start | bytes 1769480 | tf_op jit(solution)/shard_map/ppermute | solution.py:700
  273.5 18.7 %collective-permute-start.65 = (bf16[384,768]{1,0:T(8,128)(2,1)S(1)}, bf16[384,768]{1,0:T(8,128)(2,1)S(1)}, u32[]{:S(2)}, u32[]{:S(2)}) collective-permute-start(bf16[384,768]{1,0:T(8,128)(2,1)S(1)} %bitcast.52), channel_id=1, source_target_pairs={{0,8},{2,10},{4,12},{6,14},{24,16},{26,18},{28,20},{30,22},{1,9},{... | collective-permute-start | bytes 1769480 | tf_op jit(solution)/shard_map/ppermute | solution.py:700
  297.6 26.1 %collective-permute-start.70 = (bf16[384,768]{1,0:T(8,128)(2,1)}, bf16[384,768]{1,0:T(8,128)(2,1)}, u32[]{:S(2)}, u32[]{:S(2)}) collective-permute-start(bf16[384,768]{1,0:T(8,128)(2,1)} %fusion.4), channel_id=1, source_target_pairs={{8,24},{10,26},{12,28},{14,30},{9,25},{11,27},{13,29},{15,31}} | collective-permute-start | bytes 1769480 | tf_op jit(solution)/shard_map/ppermute | solution.py:700
  300.0 23.7 %collective-permute-start.69 = (bf16[384,768]{1,0:T(8,128)(2,1)}, bf16[384,768]{1,0:T(8,128)(2,1)}, u32[]{:S(2)}, u32[]{:S(2)}) collective-permute-start(bf16[384,768]{1,0:T(8,128)(2,1)} %fusion.3), channel_id=1, source_target_pairs={{16,8},{18,10},{20,12},{22,14},{17,9},{19,11},{21,13},{23,15}} | collective-permute-start | bytes 1769480 | tf_op jit(solution)/shard_map/ppermute | solution.py:700
  301.5 22.2 %collective-permute-start.68 = (bf16[384,768]{1,0:T(8,128)(2,1)}, bf16[384,768]{1,0:T(8,128)(2,1)}, u32[]{:S(2)}, u32[]{:S(2)}) collective-permute-start(bf16[384,768]{1,0:T(8,128)(2,1)} %bitcast.17), channel_id=1, source_target_pairs={{8,0},{10,2},{12,4},{14,6},{24,16},{26,18},{28,20},{30,22},{9,1},{... | collective-permute-start | bytes 1769480 | tf_op jit(solution)/shard_map/ppermute | solution.py:700
  325.5 25.1 %collective-permute-start.75 = (bf16[384,768]{1,0:T(8,128)(2,1)S(1)}, bf16[384,768]{1,0:T(8,128)(2,1)S(1)}, u32[]{:S(2)}, u32[]{:S(2)}) collective-permute-start(bf16[384,768]{1,0:T(8,128)(2,1)S(1)} %fusion.2), channel_id=1, source_target_pairs={{16,0},{18,2},{20,4},{22,6},{17,1},{19,3},{21,5},{23,7}} | collective-permute-start | bytes 1769480 | tf_op jit(solution)/shard_map/ppermute | solution.py:700
  (166 other events, 1420.4 us)
where the time goes:
time: 360 us; the launch traced here: 356 us
  Pallas kernels  116 us (32%)
  starting transfers between devices  97.4 us (27%)
  waiting for transfers between devices  97.1 us (27%)
  other arithmetic  25.3 us (7%)
  local copies, waits for them, and re-layouts  17.3 us (5%)
    pallas_call x9, Pallas kernels, run_kernel(): pl.pallas_call(call, name=body.__name__, out_shape=outs, in_specs=[pl.Blo...  108 us
    ppermute x16, waiting for transfers between devices, over_y(): return lax.ppermute(value, 'cols', swap_pairs(self.count, 2))  46.5 us
    ppermute x16, starting transfers between devices, over_z(): return lax.ppermute(value, 'cols', full)  44.7 us
    ppermute x16, waiting for transfers between devices, over_z(): return lax.ppermute(value, 'cols', full)  30 us
    ppermute x16, starting transfers between devices, over_y(): return lax.ppermute(value, 'cols', swap_pairs(self.count, 2))  20 us
    ppermute x16, starting transfers between devices, over_x(): return lax.ppermute(value, 'fsdp', [(0, 1), (1, 0)])  15.5 us
    unnamed x238, local copies, waits for them, and re-layouts  12.1 us
    ppermute x27, starting transfers between devices, over_core(): return lax.ppermute(value, 'cols', swap_pairs(self.count, 1))  11.1 us
  transfers between devices with their start and end apart: 79, of which 32 were waited for; matrix products, arithmetic and copies ran while one was open for 7% of the time, Pallas kernels for 22%

commit v1 on v0

--- a/solution.py
+++ b/solution.py
@@ -646,7 +646,7 @@
         out_specs=tuple(
             pl.BlockSpec((*shape, width), lambda j: (0, 0, j)) for shape, _d in shapes
         ),
-        compiler_params=pltpu.CompilerParams(vmem_limit_bytes=24 << 20),
+        compiler_params=pltpu.CompilerParams(vmem_limit_bytes=16 << 20),
         cost_estimate=pl.CostEstimate(
             flops=int(8 * PER_MICRO), bytes_accessed=moved, transcendentals=0
         ),

time: 360 us -> 359 us (level)
    unnamed x238 -> x230, local copies, waits for them, and re-layouts: 12.1 us -> 12.7 us
  transfers between devices with their start and end apart: 79 -> 79, of which waited for: 32 -> 31; matrix products, arithmetic and copies ran while one was open for 7% -> 7% of each run, Pallas kernels for 22% -> 22%
where the time goes in v1:
time: 359 us; the launch traced here: 355 us
  Pallas kernels  118 us (33%)
  waiting for transfers between devices  97 us (27%)
  starting transfers between devices  95.5 us (27%)
  other arithmetic  23.8 us (7%)
  local copies, waits for them, and re-layouts  17.8 us (5%)
    pallas_call x9, Pallas kernels, run_kernel(): pl.pallas_call(call, name=body.__name__, out_shape=outs, in_specs=[pl.Blo...  108 us
    ppermute x16, waiting for transfers between devices, over_y(): return lax.ppermute(value, 'cols', swap_pairs(self.count, 2))  45.3 us
    ppermute x16, starting transfers between devices, over_z(): return lax.ppermute(value, 'cols', full)  42.9 us
    ppermute x16, waiting for transfers between devices, over_z(): return lax.ppermute(value, 'cols', full)  30.1 us
    ppermute x16, starting transfers between devices, over_y(): return lax.ppermute(value, 'cols', swap_pairs(self.count, 2))  20.1 us
    ppermute x16, starting transfers between devices, over_x(): return lax.ppermute(value, 'fsdp', [(0, 1), (1, 0)])  15.5 us
    unnamed x230, local copies, waits for them, and re-layouts  12.7 us
    ppermute x16, waiting for transfers between devices, over_x(): return lax.ppermute(value, 'fsdp', [(0, 1), (1, 0)])  11 us
  transfers between devices with their start and end apart: 79, of which 31 were waited for; matrix products, arithmetic and copies ran while one was open for 7% of the time, Pallas kernels for 22%

profile of v1, /device:TPU:0, one launch (start us, length us, event | category | flops | bytes accessed | tf_op | source)
XLA Modules:
  0.0 355.1 jit_solution(17442531474620878849)
XLA Ops:
  3.0 3.0 collective-permute-start.3
  8.8 5.4 %collective-permute-start = (bf16[400,768]{1,0:T(8,128)(2,1)S(1)}, bf16[400,768]{1,0:T(8,128)(2,1)}, u32[]{:S(2)}, u32[]{:S(2)}) collective-permute-start(bf16[400,768]{1,0:T(8,128)(2,1)S(1)} %pad_maximum_fusion.refs_0_), channel_id=1, source_target_pairs={{0,8},{2,10},{4,12},{6,14},{8,16},{10,18},{12,20},{14,22},{16,24},... | collective-permute-start | bytes 1843208 | tf_op jit(solution)/shard_map/ppermute | solution.py:700
  14.2 5.7 %collective-permute-done.3.refs_2_ = bf16[400,768]{1,0:T(8,128)(2,1)S(1)} collective-permute-done((bf16[400,768]{1,0:T(8,128)(2,1)S(1)}, bf16[400,768]{1,0:T(8,128)(2,1)S(1)}, u32[]{:S(2)}, u32[]{:S(2)}) %collective-permute-start.3) | collective-permute-done | bytes 614432 | tf_op jit(solution)/shard_map/ppermute | solution.py:692
  21.3 3.1 collective-permute-done.1
  30.5 4.7 %collective-permute-start.9 = (bf16[400,768]{1,0:T(8,128)(2,1)S(1)}, bf16[400,768]{1,0:T(8,128)(2,1)S(1)}, u32[]{:S(2)}, u32[]{:S(2)}) collective-permute-start(bf16[400,768]{1,0:T(8,128)(2,1)S(1)} %broadcast_select_fusion.refs_10_), channel_id=1, source_target_pairs={{0,4},{2,6},{4,0},{6,2},{8,12},{10,14},{12,8},{14,10},{16,20},{18,... | collective-permute-start | bytes 1843208 | tf_op jit(solution)/shard_map/ppermute | solution.py:692
  39.5 5.7 %collective-permute-start.16 = (bf16[400,768]{1,0:T(8,128)(2,1)S(1)}, bf16[400,768]{1,0:T(8,128)(2,1)S(1)}, u32[]{:S(2)}, u32[]{:S(2)}) collective-permute-start(bf16[400,768]{1,0:T(8,128)(2,1)S(1)} %pad_maximum_fusion.refs_0_), channel_id=1, source_target_pairs={{0,2},{2,0},{4,6},{6,4},{8,10},{10,8},{12,14},{14,12},{16,18},{18,... | collective-permute-start | bytes 1843208 | tf_op jit(solution)/shard_map/ppermute | solution.py:695
  45.2 8.9 %collective-permute-done.9.refs_12_ = bf16[400,768]{1,0:T(8,128)(2,1)S(1)} collective-permute-done((bf16[400,768]{1,0:T(8,128)(2,1)S(1)}, bf16[400,768]{1,0:T(8,128)(2,1)S(1)}, u32[]{:S(2)}, u32[]{:S(2)}) %collective-permute-start.9) | collective-permute-done | bytes 614432 | tf_op jit(solution)/shard_map/ppermute | solution.py:692
  54.7 5.3 %collective-permute-done.5 = bf16[400,768]{1,0:T(8,128)(2,1)} collective-permute-done((bf16[400,768]{1,0:T(8,128)(2,1)}, bf16[400,768]{1,0:T(8,128)(2,1)}, u32[]{:S(2)}, u32[]{:S(2)}) %collective-permute-start.5) | collective-permute-done | bytes 614432 | tf_op jit(solution)/shard_map/ppermute | solution.py:700
  65.4 5.3 %collective-permute-done.14.refs_13_ = bf16[192,768]{1,0:T(8,128)(2,1)S(1)} collective-permute-done((bf16[192,768]{1,0:T(8,128)(2,1)S(1)}, bf16[192,768]{1,0:T(8,128)(2,1)S(1)}, u32[]{:S(2)}, u32[]{:S(2)}) %collective-permute-start.14) | collective-permute-done | bytes 294944 | tf_op jit(solution)/shard_map/ppermute | solution.py:692
  73.2 3.1 collective-permute-done.13
  82.8 9.6 %collective-permute-done.22.refs_22_ = bf16[400,768]{1,0:T(8,128)(2,1)S(1)} collective-permute-done((bf16[400,768]{1,0:T(8,128)(2,1)S(1)}, bf16[400,768]{1,0:T(8,128)(2,1)S(1)}, u32[]{:S(2)}, u32[]{:S(2)}) %collective-permute-start.22) | collective-permute-done | bytes 614432 | tf_op jit(solution)/shard_map/ppermute | solution.py:692
  99.4 5.0 %collective-permute-done.28.refs_23_ = bf16[192,768]{1,0:T(8,128)(2,1)S(1)} collective-permute-done((bf16[192,768]{1,0:T(8,128)(2,1)S(1)}, bf16[192,768]{1,0:T(8,128)(2,1)S(1)}, u32[]{:S(2)}, u32[]{:S(2)}) %collective-permute-start.28) | collective-permute-done | bytes 294944 | tf_op jit(solution)/shard_map/ppermute | solution.py:692
  110.7 10.8 %row_project.1 = (bf16[8,128,768]{2,1,0:T(8,128)(2,1)}, bf16[8,64,768]{2,1,0:T(8,128)(2,1)}, bf16[8,128,768]{2,1,0:T(8,128)(2,1)}, bf16[8,128,768]{2,1,0:T(8,128)(2,1)}, f32[3,768]{1,0:T(4,128)}) custom-call(f32[2,5]{1,0:T(2,128)} %pad_maximum_fusion.3.scal, s32[4]{0:T(128)} %pad_add_fusion.place, bf16[8,64,768]{2,1,0:T(8,128)(2,1)} %bitcast.46, ...), custom_call_target="tpu_custom_call" | custom-call | flops 10924999680 | bytes 7087104 | tf_op jit(solution)/shard_map/row_project/pallas_call | solution.py:568
  126.8 7.5 %row_attend.1 = (f32[2,6,128,128]{3,2,1,0:T(8,128)}, bf16[8,64,768]{2,1,0:T(8,128)(2,1)}, f32[8,64,768]{2,1,0:T(8,128)}, bf16[8,64,768]{2,1,0:T(8,128)(2,1)}) custom-call(f32[2,5]{1,0:T(2,128)} %pad_maximum_fusion.3.scal, s32[4]{0:T(128)} %pad_add_fusion.place, bf16[8,64,768]{2,1,0:T(8,128)(2,1)} %bitcast.47, bf16[8,64,768]{2,1,0:T(8,128)(2,1)} %get-tuple-element.214.q, ...), custom_call_target="tpu_custom_call" | custom-call | flops 14375000064 | bytes 8725504 | tf_op jit(solution)/shard_map/row_attend/pallas_call | solution.py:568
  137.3 11.9 %col_forward.1 = (bf16[8,64,768]{2,1,0:T(8,128)(2,1)}, bf16[8,64,768]{2,1,0:T(8,128)(2,1)}, bf16[8,64,768]{2,1,0:T(8,128)(2,1)}, f32[8,256,128]{2,1,0:T(8,128)},...) custom-call(f32[2,5]{1,0:T(2,128)} %pad_maximum_fusion.3.scal, ...), custom_call_target="tpu_custom_call" | custom-call | flops 17824999424 | bytes 8922112 | tf_op jit(solution)/shard_map/col_forward/pallas_call | solution.py:568
  149.2 23.1 %feed_forward.1 = (bf16[8,64,768]{2,1,0:T(8,128)(2,1)}, f32[8,64,768]{2,1,0:T(8,128)}, f32[1,768]{1,0:T(1,128)}, bf16[2,384,768]{2,1,0:T(8,128)(2,1)}, bf16[2,38...) custom-call(f32[2,5]{1,0:T(2,128)} %pad_maximum_fusion.3.scal, ...), custom_call_target="tpu_custom_call" | custom-call | flops 29899999232 | bytes 14954496 | tf_op jit(solution)/shard_map/feed_forward/pallas_call | solution.py:568
  172.5 2.9 collective-permute-done.44.got
  180.9 9.4 %col_attend_back.1 = (bf16[8,64,768]{2,1,0:T(8,128)(2,1)}, bf16[8,64,768]{2,1,0:T(8,128)(2,1)}, bf16[8,64,768]{2,1,0:T(8,128)(2,1)}) custom-call(f32[2,5]{1,0:T(2,128)S(1)} %copy-done.23, s32[4]{0:T(128)S(1)} %copy-done.24, f32[8,64,768]{2,1,0:T(8,128)} %get-tuple-element.231.e2, bf16[8,64,768]{2,1,0:T(8,128)(2,1)} %get-tuple-element.232.q2, ...), custom_call_target="tpu_custom_call" | custom-call | flops 12074999808 | bytes 7340032 | tf_op jit(solution)/shard_map/col_attend_back/pallas_call | solution.py:568
  190.3 3.1 collective-permute-done.46.half_a
  197.5 12.7 %col_project_back.1 = (f32[8,64,768]{2,1,0:T(8,128)}, f32[1,768]{1,0:T(1,128)S(1)}, bf16[1,384,768]{2,1,0:T(8,128)(2,1)S(1)}, bf16[1,384,768]{2,1,0:T(8,128)(2,1...) custom-call(f32[2,5]{1,0:T(2,128)S(1)} %copy-done.23, ...), custom_call_target="tpu_custom_call" | custom-call | flops 13224999936 | bytes 13381632 | tf_op jit(solution)/shard_map/col_project_back/pallas_call | solution.py:568
  218.3 6.0 %collective-permute-start.57 = (bf16[384,768]{1,0:T(8,128)(2,1)}, bf16[384,768]{1,0:T(8,128)(2,1)}, u32[]{:S(2)}, u32[]{:S(2)}) collective-permute-start(bf16[384,768]{1,0:T(8,128)(2,1)} %bitcast.12), channel_id=1, source_target_pairs={{0,8},{2,10},{4,12},{6,14},{24,16},{26,18},{28,20},{30,22},{1,9},{... | collective-permute-start | bytes 1769480 | tf_op jit(solution)/shard_map/ppermute | solution.py:700
  224.3 18.9 %row_backward.1 = (bf16[8,64,768]{2,1,0:T(8,128)(2,1)}, bf16[8,128,768]{2,1,0:T(8,128)(2,1)}, bf16[8,128,768]{2,1,0:T(8,128)(2,1)}, bf16[1,384,768]{2,1,0:T(8,12...) custom-call(f32[2,5]{1,0:T(2,128)S(1)} %copy-done.23, ...), custom_call_target="tpu_custom_call" | custom-call | flops 23000000512 | bytes 17301504 | tf_op jit(solution)/shard_map/row_backward/pallas_call | solution.py:568
  259.8 7.8 %collective-permute-start.66 = (bf16[384,768]{1,0:T(8,128)(2,1)}, bf16[384,768]{1,0:T(8,128)(2,1)S(1)}, u32[]{:S(2)}, u32[]{:S(2)}) collective-permute-start(bf16[384,768]{1,0:T(8,128)(2,1)} %bitcast.13), channel_id=1, source_target_pairs={{0,8},{2,10},{4,12},{6,14},{16,24},{18,26},{20,28},{22,30},{1,9},{... | collective-permute-start | bytes 1769480 | tf_op jit(solution)/shard_map/ppermute | solution.py:700
  267.6 3.6 %collective-permute-done.60.from_x = bf16[1,384,768]{2,1,0:T(8,128)(2,1)S(1)} collective-permute-done((bf16[1,384,768]{2,1,0:T(8,128)(2,1)S(1)}, bf16[1,384,768]{2,1,0:T(8,128)(2,1)S(1)}, u32[]{:S(2)}, u32[]{:S(2)}) %collective-permute-start.60) | collective-permute-done | bytes 589856 | tf_op jit(solution)/shard_map/ppermute | solution.py:689
  274.3 4.5 %collective-permute-start.65 = (bf16[384,768]{1,0:T(8,128)(2,1)}, bf16[384,768]{1,0:T(8,128)(2,1)S(1)}, u32[]{:S(2)}, u32[]{:S(2)}) collective-permute-start(bf16[384,768]{1,0:T(8,128)(2,1)} %bitcast.15), channel_id=1, source_target_pairs={{0,8},{2,10},{4,12},{6,14},{24,16},{26,18},{28,20},{30,22},{1,9},{... | collective-permute-start | bytes 1769480 | tf_op jit(solution)/shard_map/ppermute | solution.py:700
  281.3 10.5 %input_project.1 = (f32[8,64,768]{2,1,0:T(8,128)}, bf16[8,32,768]{2,1,0:T(8,128)(2,1)S(1)}, bf16[8,32,768]{2,1,0:T(8,128)(2,1)S(1)}, f32[1,768]{1,0:T(1,128)S(1)}) custom-call(f32[2,5]{1,0:T(2,128)S(1)} %copy-done.23, s32[4]{0:T(128)S(1)} %copy-done.24, bf16[8,64,768]{2,1,0:T(8,128)(2,1)} %get-tuple-element.306.dq, ...), custom_call_target="tpu_custom_call" | custom-call | flops 9200000000 | bytes 7867392 | tf_op jit(solution)/shard_map/input_project/pallas_call | solution.py:568
  305.7 3.1 collective-permute-done.72
  309.6 2.9 collective-permute-done.73
  313.2 5.0 %collective-permute-start.74 = (f32[18,128]{1,0:T(8,128)S(1)}, f32[18,128]{1,0:T(8,128)S(1)}, u32[]{:S(2)}, u32[]{:S(2)}) collective-permute-start(f32[18,128]{1,0:T(8,128)S(1)} %add.163), channel_id=1, source_target_pairs={{0,8},{2,10},{4,12},{6,14},{8,0},{10,2},{12,4},{14,6},{16,24},{18,... | collective-permute-start | bytes 27656 | tf_op jit(solution)/shard_map/ppermute | solution.py:700
  327.3 3.2 input_finish.1
  332.9 16.7 %collective-permute-done.75 = bf16[384,768]{1,0:T(8,128)(2,1)S(1)} collective-permute-done((bf16[384,768]{1,0:T(8,128)(2,1)S(1)}, bf16[384,768]{1,0:T(8,128)(2,1)S(1)}, u32[]{:S(2)}, u32[]{:S(2)}) %collective-permute-start.75) | collective-permute-done | bytes 589856 | tf_op jit(solution)/shard_map/ppermute | solution.py:700
  349.6 3.9 %fusion.7 = (bf16[384,768]{1,0:T(8,128)(2,1)}, f32[384,768]{1,0:T(8,128)}, f32[384,768]{1,0:T(8,128)}, f32[384,768]{1,0:T(8,128)}) fusion(f32[384,768]{1,0:T(8,128)S(1)} %copy-done.95, f32[384,768]{1,0:T(8,128)S(1)} %copy-done.100, f32[384,768]{1,0:T(8,128)S(1)} %copy-done.101, f32[384,768]{1,0:T(8,128)S(1)} %select_select_fusion, ...), kind=kLoop, calls=%fused_computation.39 | loop fusion | flops 6193152 | bytes 11206657 | tf_op jit(solution)/shard_map/convert_element_type | solution.py:1152
  (420 shorter events, 120.3 us)
Async XLA Ops:
  3.0 16.9 %collective-permute-start.3 = (bf16[400,768]{1,0:T(8,128)(2,1)S(1)}, bf16[400,768]{1,0:T(8,128)(2,1)S(1)}, u32[]{:S(2)}, u32[]{:S(2)}) collective-permute-start(bf16[400,768]{1,0:T(8,128)(2,1)S(1)} %pad_maximum_fusion.refs_0_), channel_id=1, source_target_pairs={{0,4},{2,6},{4,0},{6,2},{8,12},{10,14},{12,8},{14,10},{16,20},{18,... | collective-permute-start | bytes 1843208 | tf_op jit(solution)/shard_map/ppermute | solution.py:692
  6.0 15.3 %collective-permute-start.2 = (bf16[400,768]{1,0:T(8,128)(2,1)S(1)}, bf16[400,768]{1,0:T(8,128)(2,1)S(1)}, u32[]{:S(2)}, u32[]{:S(2)}) collective-permute-start(bf16[400,768]{1,0:T(8,128)(2,1)S(1)} %pad_maximum_fusion.refs_0_), channel_id=1, source_target_pairs={{0,1},{1,0},{2,3},{3,2},{4,5},{5,4},{6,7},{7,6},{8,9},{9,8},{10,11... | collective-permute-start | bytes 1843208 | tf_op jit(solution)/shard_map/ppermute | solution.py:689
  7.5 16.9 %collective-permute-start.1 = (bf16[400,768]{1,0:T(8,128)(2,1)S(1)}, bf16[400,768]{1,0:T(8,128)(2,1)S(1)}, u32[]{:S(2)}, u32[]{:S(2)}) collective-permute-start(bf16[400,768]{1,0:T(8,128)(2,1)S(1)} %pad_maximum_fusion.refs_0_), channel_id=1, source_target_pairs={{24,16},{26,18},{28,20},{30,22},{16,8},{18,10},{20,12},{22,14},{8,... | collective-permute-start | bytes 1843208 | tf_op jit(solution)/shard_map/ppermute | solution.py:700
  8.8 16.8 %collective-permute-start = (bf16[400,768]{1,0:T(8,128)(2,1)S(1)}, bf16[400,768]{1,0:T(8,128)(2,1)}, u32[]{:S(2)}, u32[]{:S(2)}) collective-permute-start(bf16[400,768]{1,0:T(8,128)(2,1)S(1)} %pad_maximum_fusion.refs_0_), channel_id=1, source_target_pairs={{0,8},{2,10},{4,12},{6,14},{8,16},{10,18},{12,20},{14,22},{16,24},... | collective-permute-start | bytes 1843208 | tf_op jit(solution)/shard_map/ppermute | solution.py:700
  30.5 23.6 %collective-permute-start.9 = (bf16[400,768]{1,0:T(8,128)(2,1)S(1)}, bf16[400,768]{1,0:T(8,128)(2,1)S(1)}, u32[]{:S(2)}, u32[]{:S(2)}) collective-permute-start(bf16[400,768]{1,0:T(8,128)(2,1)S(1)} %broadcast_select_fusion.refs_10_), channel_id=1, source_target_pairs={{0,4},{2,6},{4,0},{6,2},{8,12},{10,14},{12,8},{14,10},{16,20},{18,... | collective-permute-start | bytes 1843208 | tf_op jit(solution)/shard_map/ppermute | solution.py:692
  35.2 18.9 %collective-permute-start.8 = (bf16[400,768]{1,0:T(8,128)(2,1)S(1)}, bf16[400,768]{1,0:T(8,128)(2,1)S(1)}, u32[]{:S(2)}, u32[]{:S(2)}) collective-permute-start(bf16[400,768]{1,0:T(8,128)(2,1)S(1)} %broadcast_select_fusion.refs_10_), channel_id=1, source_target_pairs={{0,1},{1,0},{2,3},{3,2},{4,5},{5,4},{6,7},{7,6},{8,9},{9,8},{10,11... | collective-permute-start | bytes 1843208 | tf_op jit(solution)/shard_map/ppermute | solution.py:689
  36.6 18.0 %collective-permute-start.4 = (bf16[400,768]{1,0:T(8,128)(2,1)}, bf16[400,768]{1,0:T(8,128)(2,1)}, u32[]{:S(2)}, u32[]{:S(2)}) collective-permute-start(bf16[400,768]{1,0:T(8,128)(2,1)} %collective-permute-done), channel_id=1, source_target_pairs={{8,16},{10,18},{12,20},{14,22},{16,24},{18,26},{20,28},{22,30},{9,... | collective-permute-start | bytes 1843208 | tf_op jit(solution)/shard_map/ppermute | solution.py:700
  38.2 21.8 %collective-permute-start.5 = (bf16[400,768]{1,0:T(8,128)(2,1)}, bf16[400,768]{1,0:T(8,128)(2,1)}, u32[]{:S(2)}, u32[]{:S(2)}) collective-permute-start(bf16[400,768]{1,0:T(8,128)(2,1)} %copy-done.94), channel_id=1, source_target_pairs={{16,8},{18,10},{20,12},{22,14},{8,0},{10,2},{12,4},{14,6},{17,9},{... | collective-permute-start | bytes 1843208 | tf_op jit(solution)/shard_map/ppermute | solution.py:700
  39.5 23.8 %collective-permute-start.16 = (bf16[400,768]{1,0:T(8,128)(2,1)S(1)}, bf16[400,768]{1,0:T(8,128)(2,1)S(1)}, u32[]{:S(2)}, u32[]{:S(2)}) collective-permute-start(bf16[400,768]{1,0:T(8,128)(2,1)S(1)} %pad_maximum_fusion.refs_0_), channel_id=1, source_target_pairs={{0,2},{2,0},{4,6},{6,4},{8,10},{10,8},{12,14},{14,12},{16,18},{18,... | collective-permute-start | bytes 1843208 | tf_op jit(solution)/shard_map/ppermute | solution.py:695
  60.0 16.4 %collective-permute-start.13 = (bf16[400,768]{1,0:T(8,128)(2,1)}, bf16[400,768]{1,0:T(8,128)(2,1)}, u32[]{:S(2)}, u32[]{:S(2)}) collective-permute-start(bf16[400,768]{1,0:T(8,128)(2,1)} %collective-permute-done.5), channel_id=1, source_target_pairs={{8,0},{10,2},{12,4},{14,6},{9,1},{11,3},{13,5},{15,7}} | collective-permute-start | bytes 1843208 | tf_op jit(solution)/shard_map/ppermute | solution.py:700
  81.1 18.3 %collective-permute-start.30 = (bf16[400,768]{1,0:T(8,128)(2,1)S(1)}, bf16[400,768]{1,0:T(8,128)(2,1)}, u32[]{:S(2)}, u32[]{:S(2)}) collective-permute-start(bf16[400,768]{1,0:T(8,128)(2,1)S(1)} %pad_maximum_fusion.1.refs_20_), channel_id=1, source_target_pairs={{0,2},{2,0},{4,6},{6,4},{8,10},{10,8},{12,14},{14,12},{16,18},{18,... | collective-permute-start | bytes 1843208 | tf_op jit(solution)/shard_map/ppermute | solution.py:695
  106.4 28.5 %collective-permute-start.39 = (bf16[400,768]{1,0:T(8,128)(2,1)}, bf16[400,768]{1,0:T(8,128)(2,1)}, u32[]{:S(2)}, u32[]{:S(2)}) collective-permute-start(bf16[400,768]{1,0:T(8,128)(2,1)} %select_select_fusion.1.refs_30_), channel_id=1, source_target_pairs={{0,2},{2,0},{4,6},{6,4},{8,10},{10,8},{12,14},{14,12},{16,18},{18,... | collective-permute-start | bytes 1843208 | tf_op jit(solution)/shard_map/ppermute | solution.py:695
  106.5 16.4 %collective-permute-start.36 = (bf16[400,768]{1,0:T(8,128)(2,1)}, bf16[400,768]{1,0:T(8,128)(2,1)S(1)}, u32[]{:S(2)}, u32[]{:S(2)}) collective-permute-start(bf16[400,768]{1,0:T(8,128)(2,1)} %select_select_fusion.1.refs_30_), channel_id=1, source_target_pairs={{0,4},{2,6},{4,0},{6,2},{8,12},{10,14},{12,8},{14,10},{16,20},{18,... | collective-permute-start | bytes 1843208 | tf_op jit(solution)/shard_map/ppermute | solution.py:692
  107.8 16.1 %collective-permute-start.35 = (bf16[400,768]{1,0:T(8,128)(2,1)}, bf16[400,768]{1,0:T(8,128)(2,1)S(1)}, u32[]{:S(2)}, u32[]{:S(2)}) collective-permute-start(bf16[400,768]{1,0:T(8,128)(2,1)} %select_select_fusion.1.refs_30_), channel_id=1, source_target_pairs={{0,1},{1,0},{2,3},{3,2},{4,5},{5,4},{6,7},{7,6},{8,9},{9,8},{10,11... | collective-permute-start | bytes 1843208 | tf_op jit(solution)/shard_map/ppermute | solution.py:689
  177.7 16.8 %collective-permute-start.45 = (bf16[3,2,384,768]{3,2,1,0:T(8,128)(2,1)}, bf16[3,2,384,768]{3,2,1,0:T(8,128)(2,1)S(1)}, u32[]{:S(2)}, u32[]{:S(2)}) collective-permute-start(bf16[3,2,384,768]{3,2,1,0:T(8,128)(2,1)} %get-tuple-element.239), channel_id=1, source_target_pairs={{0,2},{2,0},{4,6},{6,4},{8,10},{10,8},{12,14},{14,12},{16,18},{18,... | collective-permute-start | bytes 10616840 | tf_op jit(solution)/shard_map/ppermute | solution.py:695
  177.9 15.6 %collective-permute-start.46 = (bf16[2,192,768]{2,1,0:T(8,128)(2,1)S(1)}, bf16[2,192,768]{2,1,0:T(8,128)(2,1)S(1)}, u32[]{:S(2)}, u32[]{:S(2)}) collective-permute-start(bf16[2,192,768]{2,1,0:T(8,128)(2,1)S(1)} %get-tuple-element.229), channel_id=1, source_target_pairs={{0,4},{2,6},{4,0},{6,2},{8,12},{10,14},{12,8},{14,10},{16,20},{18,... | collective-permute-start | bytes 1769480 | tf_op jit(solution)/shard_map/ppermute | solution.py:692
  179.1 15.3 %collective-permute-start.47 = (bf16[2,192,768]{2,1,0:T(8,128)(2,1)S(1)}, bf16[2,192,768]{2,1,0:T(8,128)(2,1)S(1)}, u32[]{:S(2)}, u32[]{:S(2)}) collective-permute-start(bf16[2,192,768]{2,1,0:T(8,128)(2,1)S(1)} %get-tuple-element.230), channel_id=1, source_target_pairs={{0,1},{1,0},{2,3},{3,2},{4,5},{5,4},{6,7},{7,6},{8,9},{9,8},{10,11... | collective-permute-start | bytes 1769480 | tf_op jit(solution)/shard_map/ppermute | solution.py:689
  214.2 29.9 %collective-permute-start.54 = (bf16[1,192,768]{2,1,0:T(8,128)(2,1)S(1)}, bf16[1,192,768]{2,1,0:T(8,128)(2,1)S(1)}, u32[]{:S(2)}, u32[]{:S(2)}) collective-permute-start(bf16[1,192,768]{2,1,0:T(8,128)(2,1)S(1)} %get-tuple-element.259), channel_id=1, source_target_pairs={{0,1},{1,0},{2,3},{3,2},{4,5},{5,4},{6,7},{7,6},{8,9},{9,8},{10,11... | collective-permute-start | bytes 884744 | tf_op jit(solution)/shard_map/ppermute | solution.py:689
  215.6 29.0 %collective-permute-start.55 = (bf16[1,384,768]{2,1,0:T(8,128)(2,1)S(1)}, bf16[1,384,768]{2,1,0:T(8,128)(2,1)S(1)}, u32[]{:S(2)}, u32[]{:S(2)}) collective-permute-start(bf16[1,384,768]{2,1,0:T(8,128)(2,1)S(1)} %get-tuple-element.255), channel_id=1, source_target_pairs={{0,1},{1,0},{2,3},{3,2},{4,5},{5,4},{6,7},{7,6},{8,9},{9,8},{10,11... | collective-permute-start | bytes 1769480 | tf_op jit(solution)/shard_map/ppermute | solution.py:689
  216.2 28.4 %collective-permute-start.56 = (bf16[1,384,768]{2,1,0:T(8,128)(2,1)S(1)}, bf16[1,384,768]{2,1,0:T(8,128)(2,1)S(1)}, u32[]{:S(2)}, u32[]{:S(2)}) collective-permute-start(bf16[1,384,768]{2,1,0:T(8,128)(2,1)S(1)} %get-tuple-element.256), channel_id=1, source_target_pairs={{0,4},{2,6},{4,0},{6,2},{8,12},{10,14},{12,8},{14,10},{16,20},{18,... | collective-permute-start | bytes 1769480 | tf_op jit(solution)/shard_map/ppermute | solution.py:692
  218.3 26.3 %collective-permute-start.57 = (bf16[384,768]{1,0:T(8,128)(2,1)}, bf16[384,768]{1,0:T(8,128)(2,1)}, u32[]{:S(2)}, u32[]{:S(2)}) collective-permute-start(bf16[384,768]{1,0:T(8,128)(2,1)} %bitcast.12), channel_id=1, source_target_pairs={{0,8},{2,10},{4,12},{6,14},{24,16},{26,18},{28,20},{30,22},{1,9},{... | collective-permute-start | bytes 1769480 | tf_op jit(solution)/shard_map/ppermute | solution.py:700
  224.2 20.4 %collective-permute-start.52 = (bf16[3,1,384,768]{3,2,1,0:T(8,128)(2,1)}, bf16[3,1,384,768]{3,2,1,0:T(8,128)(2,1)S(1)}, u32[]{:S(2)}, u32[]{:S(2)}) collective-permute-start(bf16[3,1,384,768]{3,2,1,0:T(8,128)(2,1)} %get-tuple-element.273), channel_id=1, source_target_pairs={{0,2},{2,0},{4,6},{6,4},{8,10},{10,8},{12,14},{14,12},{16,18},{18,... | collective-permute-start | bytes 5308424 | tf_op jit(solution)/shard_map/ppermute | solution.py:695
  248.5 22.7 %collective-permute-start.62 = (bf16[3,1,384,768]{3,2,1,0:T(8,128)(2,1)S(1)}, bf16[3,1,384,768]{3,2,1,0:T(8,128)(2,1)S(1)}, u32[]{:S(2)}, u32[]{:S(2)}) collective-permute-start(bf16[3,1,384,768]{3,2,1,0:T(8,128)(2,1)S(1)} %copy-done.111), channel_id=1, source_target_pairs={{0,2},{2,0},{4,6},{6,4},{8,10},{10,8},{12,14},{14,12},{16,18},{18,... | collective-permute-start | bytes 5308424 | tf_op jit(solution)/shard_map/ppermute | solution.py:695
  251.4 19.8 %collective-permute-start.60 = (bf16[1,384,768]{2,1,0:T(8,128)(2,1)S(1)}, bf16[1,384,768]{2,1,0:T(8,128)(2,1)S(1)}, u32[]{:S(2)}, u32[]{:S(2)}) collective-permute-start(bf16[1,384,768]{2,1,0:T(8,128)(2,1)S(1)} %get-tuple-element.278), channel_id=1, source_target_pairs={{0,1},{1,0},{2,3},{3,2},{4,5},{5,4},{6,7},{7,6},{8,9},{9,8},{10,11... | collective-permute-start | bytes 1769480 | tf_op jit(solution)/shard_map/ppermute | solution.py:689
  251.9 19.3 %collective-permute-start.61 = (bf16[1,384,768]{2,1,0:T(8,128)(2,1)S(1)}, bf16[1,384,768]{2,1,0:T(8,128)(2,1)S(1)}, u32[]{:S(2)}, u32[]{:S(2)}) collective-permute-start(bf16[1,384,768]{2,1,0:T(8,128)(2,1)S(1)} %get-tuple-element.279), channel_id=1, source_target_pairs={{0,4},{2,6},{4,0},{6,2},{8,12},{10,14},{12,8},{14,10},{16,20},{18,... | collective-permute-start | bytes 1769480 | tf_op jit(solution)/shard_map/ppermute | solution.py:692
  258.3 34.9 %collective-permute-start.67 = (bf16[384,768]{1,0:T(8,128)(2,1)}, bf16[384,768]{1,0:T(8,128)(2,1)}, u32[]{:S(2)}, u32[]{:S(2)}) collective-permute-start(bf16[384,768]{1,0:T(8,128)(2,1)} %fusion.1), channel_id=1, source_target_pairs={{8,16},{10,18},{12,20},{14,22},{9,17},{11,19},{13,21},{15,23}} | collective-permute-start | bytes 1769480 | tf_op jit(solution)/shard_map/ppermute | solution.py:700
  259.8 33.3 %collective-permute-start.66 = (bf16[384,768]{1,0:T(8,128)(2,1)}, bf16[384,768]{1,0:T(8,128)(2,1)S(1)}, u32[]{:S(2)}, u32[]{:S(2)}) collective-permute-start(bf16[384,768]{1,0:T(8,128)(2,1)} %bitcast.13), channel_id=1, source_target_pairs={{0,8},{2,10},{4,12},{6,14},{16,24},{18,26},{20,28},{22,30},{1,9},{... | collective-permute-start | bytes 1769480 | tf_op jit(solution)/shard_map/ppermute | solution.py:700
  274.3 18.8 %collective-permute-start.65 = (bf16[384,768]{1,0:T(8,128)(2,1)}, bf16[384,768]{1,0:T(8,128)(2,1)S(1)}, u32[]{:S(2)}, u32[]{:S(2)}) collective-permute-start(bf16[384,768]{1,0:T(8,128)(2,1)} %bitcast.15), channel_id=1, source_target_pairs={{0,8},{2,10},{4,12},{6,14},{24,16},{26,18},{28,20},{30,22},{1,9},{... | collective-permute-start | bytes 1769480 | tf_op jit(solution)/shard_map/ppermute | solution.py:700
  296.5 26.3 %collective-permute-start.70 = (bf16[384,768]{1,0:T(8,128)(2,1)}, bf16[384,768]{1,0:T(8,128)(2,1)}, u32[]{:S(2)}, u32[]{:S(2)}) collective-permute-start(bf16[384,768]{1,0:T(8,128)(2,1)} %fusion.4), channel_id=1, source_target_pairs={{8,24},{10,26},{12,28},{14,30},{9,25},{11,27},{13,29},{15,31}} | collective-permute-start | bytes 1769480 | tf_op jit(solution)/shard_map/ppermute | solution.py:700
  299.0 23.9 %collective-permute-start.69 = (bf16[384,768]{1,0:T(8,128)(2,1)}, bf16[384,768]{1,0:T(8,128)(2,1)}, u32[]{:S(2)}, u32[]{:S(2)}) collective-permute-start(bf16[384,768]{1,0:T(8,128)(2,1)} %fusion.3), channel_id=1, source_target_pairs={{16,8},{18,10},{20,12},{22,14},{17,9},{19,11},{21,13},{23,15}} | collective-permute-start | bytes 1769480 | tf_op jit(solution)/shard_map/ppermute | solution.py:700
  300.4 22.4 %collective-permute-start.68 = (bf16[384,768]{1,0:T(8,128)(2,1)}, bf16[384,768]{1,0:T(8,128)(2,1)}, u32[]{:S(2)}, u32[]{:S(2)}) collective-permute-start(bf16[384,768]{1,0:T(8,128)(2,1)} %bitcast.17), channel_id=1, source_target_pairs={{8,0},{10,2},{12,4},{14,6},{24,16},{26,18},{28,20},{30,22},{9,1},{... | collective-permute-start | bytes 1769480 | tf_op jit(solution)/shard_map/ppermute | solution.py:700
  324.6 25.0 %collective-permute-start.75 = (bf16[384,768]{1,0:T(8,128)(2,1)S(1)}, bf16[384,768]{1,0:T(8,128)(2,1)S(1)}, u32[]{:S(2)}, u32[]{:S(2)}) collective-permute-start(bf16[384,768]{1,0:T(8,128)(2,1)S(1)} %fusion.2), channel_id=1, source_target_pairs={{16,0},{18,2},{20,4},{22,6},{17,1},{19,3},{21,5},{23,7}} | collective-permute-start | bytes 1769480 | tf_op jit(solution)/shard_map/ppermute | solution.py:700
  (162 other events, 1366.2 us)
